TPU v7x, 256 devices: a whole 4x4x8 slice. The times are simulated.
256 devices in a mesh: segment: 2 (over core), seq: 128 (over z, x, y).
Axes of the slice: x: 4, y: 4, z: 8, core: 2. Of those that a mesh axis runs over, the one named last changes fastest.
Arguments:
- tracks_in: bfloat16 [1, 128, 512, 1536], P(None, 'seq'), may hold values from -120 to 120
- w_qkv: bfloat16 [2, 1536, 2304], P('segment'), may hold values from -0.15625 to 0.15625
- w_out: bfloat16 [2, 768, 1536], P('segment'), may hold values from -0.21875 to 0.21875
- visible: int32 [1, 128, 512], P(None, 'seq'), may hold values 0 or 1
- neighbours: int32 [1, 8, 4, 2], replicated, may hold values from 0 to 3, as said below
Outputs:
- section_tokens: bfloat16 [2, 1, 128, 512, 1536], P('segment', None, 'seq')
Inputs may be any that keep to these rules, and one draw needn't show every extreme that they name: `neighbours`: each row names 2 different track blocks, none of them the row's own block.
All inputs are finite; a program needn't handle non-finite values. No bound on the sum of `visible` on one device may be relied on, other than what follows from the above.
Results may differ from a plain program's by a relative error of at most 0.0042.
Values may be sent and summed in bfloat16 or wider, within the bound.
No kernel may reach another device: no remote copies, remote signals or barrier semaphores. Data moves between devices by JAX's collectives and lax.ppermute only.
A program may use at most 128 MiB of HBM per device.

v0:
```python
import math

import jax
import jax.numpy as jnp
from jax import lax
from jax.experimental import pallas as pl
from jax.experimental.pallas import tpu as pltpu
from jax.sharding import Mesh, PartitionSpec as P

HEADS = 6
HDIM = 128
BLOCK = 128
FRAMES = 16
INNER = HEADS * HDIM
PAIR = 2 * HDIM
PAIRS = HEADS // 2
EPS = 1e-06
SCALE = 1.0 / math.sqrt(HDIM)

f32 = jnp.float32
bf16 = jnp.bfloat16


def regroup(rows, outer, inner, unit):
    to = lax.broadcasted_iota(jnp.int32, (rows, rows), 0)
    source = lax.broadcasted_iota(jnp.int32, (rows, rows), 1)
    u = to % unit
    o = (to // unit) % outer
    i = to // (unit * outer)
    return (source == o * (inner * unit) + i * unit + u).astype(bf16)


def permute_rows(one_hot, value):
    return jnp.dot(one_hot, value, preferred_element_type=f32).astype(bf16)


def spread_kernel(x_ref, p_ref, o_ref):
    o_ref[...] = permute_rows(p_ref[...], x_ref[...])


def spread(x, one_hot, columns=512):
    rows, width = x.shape
    return pl.pallas_call(
        spread_kernel,
        out_shape=jax.ShapeDtypeStruct((rows, width), bf16),
        grid=(width // columns,),
        in_specs=[
            pl.BlockSpec((rows, columns), lambda j: (0, j)),
            pl.BlockSpec((rows, rows), lambda j: (0, 0)),
        ],
        out_specs=pl.BlockSpec((rows, columns), lambda j: (0, j)),
        name="spread",
    )(x, one_hot)


def row_factor(x):
    wide = x.astype(f32)
    return lax.rsqrt(jnp.mean(wide * wide, axis=-1, keepdims=True) + EPS)


def load_qkv(w_hbm, w_buf, sem):
    copies = []
    for pair in range(PAIRS):
        for part in range(3):
            columns = pl.ds(part * INNER + pair * PAIR, PAIR)
            copies.append(
                pltpu.make_async_copy(
                    w_hbm.at[:, columns], w_buf.at[:, columns], sem.at[pair, part]
                )
            )
    for copy in copies:
        copy.start()
    return copies


def time_kernel(x_ref, w_hbm, o_ref, w_buf, sem):
    copies = load_qkv(w_hbm, w_buf, sem)
    rows = x_ref.shape[0]
    tracks = rows // FRAMES
    x = x_ref[...]
    factor = row_factor(x)
    side = FRAMES * 8
    same = (
        lax.broadcasted_iota(jnp.int32, (side, side), 0) % 8
        == lax.broadcasted_iota(jnp.int32, (side, side), 1) % 8
    )
    for pair in range(PAIRS):
        parts = []
        for part in range(3):
            copies[pair * 3 + part].wait()
            columns = pl.ds(part * INNER + pair * PAIR, PAIR)
            y = jnp.dot(x, w_buf[:, columns], preferred_element_type=f32) * factor
            parts.append(y.reshape(FRAMES, tracks, PAIR))
        for head in range(2):
            for group in range(tracks // 8):
                q, k, v = (
                    y[:, group * 8 : group * 8 + 8, head * HDIM : head * HDIM + HDIM]
                    .reshape(side, HDIM)
                    .astype(bf16)
                    for y in parts
                )
                scores = lax.dot_general(
                    q, k, (((1,), (1,)), ((), ())), preferred_element_type=f32
                )
                e = jnp.where(same, jnp.exp(scores * SCALE), 0.0)
                weights = (e / jnp.sum(e, axis=-1, keepdims=True)).astype(bf16)
                mixed = jnp.dot(weights, v, preferred_element_type=f32)
                at = (pair * 2 + head) * HDIM
                o_ref[:, group * 8 : group * 8 + 8, at : at + HDIM] = mixed.reshape(
                    FRAMES, 8, HDIM
                ).astype(bf16)


def time_section(x, w):
    rows, width = x.shape
    return pl.pallas_call(
        time_kernel,
        out_shape=jax.ShapeDtypeStruct((FRAMES, rows // FRAMES, INNER), bf16),
        in_specs=[
            pl.BlockSpec(memory_space=pltpu.VMEM),
            pl.BlockSpec(memory_space=pl.ANY),
        ],
        out_specs=pl.BlockSpec(memory_space=pltpu.VMEM),
        scratch_shapes=[
            pltpu.VMEM((width, 3 * INNER), bf16),
            pltpu.SemaphoreType.DMA((PAIRS, 3)),
        ],
        compiler_params=pltpu.CompilerParams(vmem_limit_bytes=40 << 20),
        name="time_section",
    )(x, w)


def finish_kernel(x_ref, m_ref, w_ref, p_ref, o_ref):
    delta = jnp.dot(m_ref[...], w_ref[...], preferred_element_type=f32)
    first = (x_ref[...].astype(f32) + delta).astype(bf16)
    o_ref[...] = permute_rows(p_ref[...], first)


def finish_first(x, mixed, w, one_hot, columns=512):
    rows, width = x.shape
    return pl.pallas_call(
        finish_kernel,
        out_shape=jax.ShapeDtypeStruct((rows, width), bf16),
        grid=(width // columns,),
        in_specs=[
            pl.BlockSpec((rows, columns), lambda j: (0, j)),
            pl.BlockSpec((rows, INNER), lambda j: (0, 0)),
            pl.BlockSpec((INNER, columns), lambda j: (0, j)),
            pl.BlockSpec((rows, rows), lambda j: (0, 0)),
        ],
        out_specs=pl.BlockSpec((rows, columns), lambda j: (0, j)),
        name="finish_first",
    )(x, mixed, w, one_hot)


def track_kernel(
    lists, x_ref, m_ref, p_ref, seen_ref, w0_hbm, wq_hbm, w1_hbm, o_ref,
    w0, wq, w1, first, qkv, mixed1, sem, sem_out,
):
    copy_0 = pltpu.make_async_copy(w0_hbm, w0, sem_out.at[0])
    copy_0.start()
    copies = load_qkv(wq_hbm, wq, sem)
    copy_1 = pltpu.make_async_copy(w1_hbm, w1, sem_out.at[1])
    copy_1.start()
    rows = x_ref.shape[0]
    blocks = rows // BLOCK
    mixed0 = permute_rows(p_ref[...], m_ref[...])
    copy_0.wait()
    delta = jnp.dot(mixed0, w0[...], preferred_element_type=f32)
    first[...] = (x_ref[...].astype(f32) + delta).astype(bf16)
    factor = row_factor(first[...])
    itself = lax.broadcasted_iota(jnp.int32, (BLOCK, BLOCK), 0) == lax.broadcasted_iota(
        jnp.int32, (BLOCK, BLOCK), 1
    )
    for pair in range(PAIRS):
        for part in range(3):
            copies[pair * 3 + part].wait()
            columns = pl.ds(part * INNER + pair * PAIR, PAIR)
            y = jnp.dot(first[...], wq[:, columns], preferred_element_type=f32) * factor
            qkv[:, columns] = y.astype(bf16)
        for block in range(blocks):
            others = [lists[block * 2], lists[block * 2 + 1]]
            places = [pl.ds(block * BLOCK, BLOCK)] + [
                pl.ds(pl.multiple_of(o * BLOCK, BLOCK), BLOCK) for o in others
            ]
            allowed = [(seen_ref[block : block + 1, :] == 1) | itself] + [
                seen_ref[pl.ds(o, 1), :] == 1 for o in others
            ]
            for head in range(2):
                at = (pair * 2 + head) * HDIM
                q = qkv[pl.ds(block * BLOCK, BLOCK), at : at + HDIM]
                es = []
                for place, allow in zip(places, allowed):
                    k = qkv[place, INNER + at : INNER + at + HDIM]
                    scores = lax.dot_general(
                        q, k, (((1,), (1,)), ((), ())), preferred_element_type=f32
                    )
                    es.append(jnp.where(allow, jnp.exp(scores * SCALE), 0.0))
                total = sum(jnp.sum(e, axis=-1, keepdims=True) for e in es)
                acc = None
                for place, e in zip(places, es):
                    v = qkv[place, 2 * INNER + at : 2 * INNER + at + HDIM]
                    part_sum = jnp.dot((e / total).astype(bf16), v, preferred_element_type=f32)
                    acc = part_sum if acc is None else acc + part_sum
                mixed1[pl.ds(block * BLOCK, BLOCK), at : at + HDIM] = acc.astype(bf16)
    copy_1.wait()
    delta = jnp.dot(mixed1[...], w1[...], preferred_element_type=f32)
    o_ref[...] = (first[...].astype(f32) + delta).astype(bf16)


def track_section(lists, x, mixed0, one_hot, seen, w_out0, w_qkv, w_out1):
    rows, width = x.shape
    vmem = pl.BlockSpec(memory_space=pltpu.VMEM)
    hbm = pl.BlockSpec(memory_space=pl.ANY)
    return pl.pallas_call(
        track_kernel,
        out_shape=jax.ShapeDtypeStruct((rows, width), bf16),
        in_specs=[pl.BlockSpec(memory_space=pltpu.SMEM), vmem, vmem, vmem, vmem, hbm, hbm, hbm],
        out_specs=vmem,
        scratch_shapes=[
            pltpu.VMEM((INNER, width), bf16),
            pltpu.VMEM((width, 3 * INNER), bf16),
            pltpu.VMEM((INNER, width), bf16),
            pltpu.VMEM((rows, width), bf16),
            pltpu.VMEM((rows, 3 * INNER), bf16),
            pltpu.VMEM((rows, INNER), bf16),
            pltpu.SemaphoreType.DMA((PAIRS, 3)),
            pltpu.SemaphoreType.DMA((2,)),
        ],
        compiler_params=pltpu.CompilerParams(vmem_limit_bytes=48 << 20),
        name="track_section",
    )(lists, x, mixed0, one_hot, seen, w_out0, w_qkv, w_out1)


def exchange(value, axis):
    return lax.all_to_all(value, axis, split_axis=0, concat_axis=0, tiled=True)


def on_device(tracks_in, w_qkv, w_out, visible, neighbours):
    segment_no = lax.axis_index("segment")
    video_no = lax.axis_index("z")
    planes = lax.axis_size("z")
    frames = lax.axis_size("plane")
    x = tracks_in[0, 0]
    rows, width = x.shape
    per_chip = rows // frames
    unit = per_chip // planes
    w_in, w_back = w_qkv[0], w_out[0]
    seen = visible[0, 0].reshape(rows // BLOCK, BLOCK)
    lists = lax.dynamic_index_in_dim(neighbours[0], video_no, 0, keepdims=False).reshape(-1)
    to_chips = regroup(rows, planes, frames, unit)
    to_tracks = regroup(rows, frames, planes, unit)
    w_back_first = lax.ppermute(w_back, "segment", [(0, 1)])

    def section_one():
        sent = spread(x, to_chips).reshape(frames, per_chip, width)
        moved = exchange(sent, "plane").reshape(rows, width)
        return moved, time_section(moved, w_in)

    def idle():
        return jnp.zeros((rows, width), bf16), jnp.zeros((frames, per_chip, INNER), bf16)

    moved, mixed0 = lax.cond(segment_no == 0, section_one, idle)
    handed = lax.ppermute(mixed0, "segment", [(0, 1)])

    def track_order():
        first = finish_first(moved, mixed0.reshape(rows, INNER), w_back, to_tracks)
        return exchange(first.reshape(planes, frames * unit, width), "z").reshape(rows, width)

    def section_two():
        back = exchange(handed, "plane").reshape(rows, INNER)
        return track_section(lists, x, back, to_tracks, seen, w_back_first, w_in, w_back)

    result = lax.cond(segment_no == 0, track_order, section_two)
    return result[None, None, None]


def solution(mesh):
    frames = FRAMES
    devices = mesh.devices.reshape(mesh.devices.shape[0], -1, frames)
    grid = Mesh(devices, ("segment", "z", "plane"))
    seq = ("z", "plane")
    return jax.shard_map(
        on_device,
        mesh=grid,
        in_specs=(
            P(None, seq, None, None),
            P("segment", None, None),
            P("segment", None, None),
            P(None, seq, None),
            P(),
        ),
        out_specs=P("segment", None, seq, None, None),
        check_vma=False,
    )
```

profile of v0, /device:TPU:1, one launch (start us, length us, event | category | flops | bytes accessed | tf_op | source)
XLA Modules:
  0.0 94.5 jit_solution(17324256028775942429)
XLA Ops:
  0.0 1.3 %collective-permute-start.1 = (bf16[768,1536]{1,0:T(8,128)(2,1)}, bf16[768,1536]{1,0:T(8,128)(2,1)}, u32[]{:S(2)}, u32[]{:S(2)}) collective-permute-start(bf16[768,1536]{1,0:T(8,128)(2,1)} %bitcast.14), channel_id=1, source_target_pairs={{0,128},{1,129},{2,130},{3,131},{4,132},{5,133},{6,134},{7,135},{8... | collective-permute-start | bytes 7077896 | tf_op jit(solution)/shard_map/ppermute | solution.py:253
  1.4 2.3 %fusion.8 = (bf16[512,512]{1,0:T(8,128)(2,1)}, bf16[512,512]{1,0:T(8,128)(2,1)}) fusion(s32[512]{0:T(512)S(1)} %get-tuple-element.100, s32[512]{0:T(512)S(1)} %get-tuple-element.102, s32[512]{0:T(512)S(1)} %get-tuple-element.99, s32[512]{0:T(512)S(1)} %get-tuple-element.101, s32[512]{0:T(512)S(1)} %get-tuple-element.98, s32[512]{0:T(512)S(1)} %get-tuple-element.108, ...), kind=kLoop, calls=%fused_computation.18 | loop fusion | flops 9175040 | bytes 1067008 | tf_op jit(solution)/shard_map/convert_element_type | solution.py:30
  3.7 0.0 copy-start
  3.7 0.0 copy-start.1
  3.7 0.0 copy-start.2
  3.7 1.3 %conditional.2 = (bf16[512,1536]{1,0:T(8,128)(2,1)}, bf16[16,32,768]{2,1,0:T(8,128)(2,1)S(1)}) conditional(s32[]{:T(128)} %convert_element_type.12, () %tuple.21, (bf16[512,1536]{1,0:T(8,128)(2,1)}, bf16[512,512]{1,0:T(8,128)(2,1)}, bf16[1536,2304]{1,0:T(8,128)(2,1)}) %tuple.44), branch_computations={%region_0.1_spmd, %region_1.2_spmd} | conditional | bytes 3145744 | solution.py:263
  3.7 0.1 broadcast.88
  3.8 1.3 %broadcast.87 = bf16[512,1536]{1,0:T(8,128)(2,1)} broadcast(bf16[]{:T(256)} %constant.92.clone), dimensions={} | broadcast | bytes 1572866 | tf_op jit(solution)/shard_map/broadcast.6
  5.0 1.3 %collective-permute-start = (bf16[16,32,768]{2,1,0:T(8,128)(2,1)S(1)}, bf16[16,32,768]{2,1,0:T(8,128)(2,1)}, u32[]{:S(2)}, u32[]{:S(2)}) collective-permute-start(bf16[16,32,768]{2,1,0:T(8,128)(2,1)S(1)} %get-tuple-element.70), channel_id=1, source_target_pairs={{0,128},{1,129},{2,130},{3,131},{4,132},{5,133},{6,134},{7,135},{8... | collective-permute-start | bytes 2359304 | tf_op jit(solution)/shard_map/ppermute | solution.py:264
  6.3 47.6 %collective-permute-done = bf16[16,32,768]{2,1,0:T(8,128)(2,1)} collective-permute-done((bf16[16,32,768]{2,1,0:T(8,128)(2,1)S(1)}, bf16[16,32,768]{2,1,0:T(8,128)(2,1)}, u32[]{:S(2)}, u32[]{:S(2)}) %collective-permute-start) | collective-permute-done | bytes 786464 | tf_op jit(solution)/shard_map/ppermute | solution.py:264
  54.0 0.0 collective-permute-done.1
  54.0 0.0 copy-done
  54.0 0.0 copy-done.1
  54.0 0.0 copy-done.2
  54.0 39.3 %conditional.3 = (bf16[1,1,1,512,1536]{4,3,2,1,0:T(8,128)(2,1)S(1)}) conditional(s32[]{:T(128)} %convert_element_type.12, (s32[]{:T(128)}, s32[1,8,4,2]{1,3,2,0:T(2,128)S(1)}, bf16[16,32,768]{2,1,0:T(8,128)(2,1)}, s32[1,1,512]{2,1,0:T(1,128)S(1)}, bf16[512,1536]{1,0:T(8,128)(2,1)}, /*index=5*/bf16[512,512]{1,0:T(8,128)(2,1)}, ...), branch_computations={%region_2.3_spmd, %region_3.4_spmd} | conditional | flops 3 | bytes 3145736 | solution.py:274
  54.0 3.8 %all-to-all-start.2 = ((bf16[16,32,768]{2,1,0:T(8,128)(2,1)}), bf16[16,32,768]{2,1,0:T(8,128)(2,1)S(1)}, u32[]{:S(2)}, u32[]{:S(2)}) async-start(bf16[16,32,768]{2,1,0:T(8,128)(2,1)} %get-tuple-element.58), calls=%async_computation.2 | async-start | bytes 1572864 | tf_op jit(solution)/shard_map/cond/branch_0_fun/all_to_all | solution.py:236
  57.8 0.1 copy.11
  57.9 0.1 reshape.20.lists
  58.0 9.9 %all-to-all-done.2 = bf16[16,32,768]{2,1,0:T(8,128)(2,1)S(1)} async-done(((bf16[16,32,768]{2,1,0:T(8,128)(2,1)}), bf16[16,32,768]{2,1,0:T(8,128)(2,1)S(1)}, u32[]{:S(2)}, u32[]{:S(2)}) %all-to-all-start.2) | async-done | bytes 786464 | tf_op jit(solution)/shard_map/cond/branch_0_fun/all_to_all | solution.py:236
  67.9 25.2 %track_section.1 = bf16[512,1536]{1,0:T(8,128)(2,1)S(1)} custom-call(s32[8]{0:T(128)S(1)} %reshape.20.lists, bf16[512,1536]{1,0:T(8,128)(2,1)} %get-tuple-element.57.x_ref, bf16[512,768]{1,0:T(8,128)(2,1)S(1)} %bitcast.11, bf16[512,512]{1,0:T(8,128)(2,1)} %get-tuple-element.59.p_ref, s32[4,128]{1,0:T(4,128)S(1)} %bitcast.24, ...), custom_call_target="tpu_custom_call" | custom-call | tf_op jit(solution)/shard_map/cond/branch_0_fun/track_section/pallas_call | solution.py:215
  93.3 1.1 %copy.19 = bf16[1,1,1,512,1536]{4,3,2,1,0:T(8,128)(2,1)} copy(bf16[1,1,1,512,1536]{4,3,2,1,0:T(8,128)(2,1)S(1)} %get-tuple-element.72) | data formatting | bytes 3145728
  (7 shorter events, 0.0 us)
Async XLA Ops:
  0.0 54.0 %collective-permute-start.1 = (bf16[768,1536]{1,0:T(8,128)(2,1)}, bf16[768,1536]{1,0:T(8,128)(2,1)}, u32[]{:S(2)}, u32[]{:S(2)}) collective-permute-start(bf16[768,1536]{1,0:T(8,128)(2,1)} %bitcast.14), channel_id=1, source_target_pairs={{0,128},{1,129},{2,130},{3,131},{4,132},{5,133},{6,134},{7,135},{8... | collective-permute-start | bytes 7077896 | tf_op jit(solution)/shard_map/ppermute | solution.py:253
  3.7 50.3 %copy-start = (bf16[1,768,1536]{2,1,0:T(8,128)(2,1)S(1)}, bf16[1,768,1536]{2,1,0:T(8,128)(2,1)}, u32[]{:S(2)}) copy-start(bf16[1,768,1536]{2,1,0:T(8,128)(2,1)} %param.11) | copy-start | bytes 7077892
  3.7 50.3 %copy-start.1 = (s32[1,8,4,2]{1,3,2,0:T(2,128)S(1)}, s32[1,8,4,2]{1,3,2,0:T(2,128)}, u32[]{:S(2)}) copy-start(s32[1,8,4,2]{1,3,2,0:T(2,128)} %param.13) | copy-start | bytes 772
  3.7 50.3 %copy-start.2 = (s32[1,1,512]{2,1,0:T(1,128)S(1)}, s32[1,1,512]{2,1,0:T(1,128)}, u32[]{:S(2)}) copy-start(s32[1,1,512]{2,1,0:T(1,128)} %param.12) | copy-start | bytes 6148
  5.0 48.9 %collective-permute-start = (bf16[16,32,768]{2,1,0:T(8,128)(2,1)S(1)}, bf16[16,32,768]{2,1,0:T(8,128)(2,1)}, u32[]{:S(2)}, u32[]{:S(2)}) collective-permute-start(bf16[16,32,768]{2,1,0:T(8,128)(2,1)S(1)} %get-tuple-element.70), channel_id=1, source_target_pairs={{0,128},{1,129},{2,130},{3,131},{4,132},{5,133},{6,134},{7,135},{8... | collective-permute-start | bytes 2359304 | tf_op jit(solution)/shard_map/ppermute | solution.py:264
  54.0 13.9 %all-to-all-start.2 = ((bf16[16,32,768]{2,1,0:T(8,128)(2,1)}), bf16[16,32,768]{2,1,0:T(8,128)(2,1)S(1)}, u32[]{:S(2)}, u32[]{:S(2)}) async-start(bf16[16,32,768]{2,1,0:T(8,128)(2,1)} %get-tuple-element.58), calls=%async_computation.2 | async-start | bytes 1572864 | tf_op jit(solution)/shard_map/cond/branch_0_fun/all_to_all | solution.py:236
where the time goes:
time: 94.8 us; the launch traced here: 94.5 us
  waiting for transfers between devices  57.6 us (61%)
  Pallas kernels  25.2 us (27%)
  starting transfers between devices  6.37 us (7%)
  local copies, waits for them, and re-layouts  2.68 us (3%)
  other arithmetic  2.35 us (2%)
    ppermute x1, waiting for transfers between devices, on_device(): handed = lax.ppermute(mixed0, 'segment', [(0, 1)])  47.6 us
    pallas_call x1, Pallas kernels, track_section(): pl.pallas_call(track_kernel, out_shape=jax.ShapeDtypeStruct((rows, width)...  25.2 us
    all_to_all x1, waiting for transfers between devices, exchange(): return lax.all_to_all(value, axis, split_axis=0, concat_axis=0, tiled=True)  9.94 us
    all_to_all x1, starting transfers between devices, exchange(): return lax.all_to_all(value, axis, split_axis=0, concat_axis=0, tiled=True)  3.81 us
    convert_element_type x1, other arithmetic, regroup(): return (source == o * (inner * unit) + i * unit + u).astype(bf16)  2.32 us
  transfers between devices with their start and end apart: 3, of which 2 were waited for; matrix products, arithmetic and copies ran while one was open for 4% of the time, Pallas kernels for 0%

commit v1 on v0

v1 whole, which is shorter than its diff:
```python
import functools
import math

import jax
import jax.numpy as jnp
from jax import lax
from jax.experimental import pallas as pl
from jax.experimental.pallas import tpu as pltpu
from jax.sharding import Mesh, PartitionSpec as P

HEADS = 6
HDIM = 128
BLOCK = 128
FRAMES = 16
UNIT = 4
INNER = HEADS * HDIM
PAIR = 2 * HDIM
PAIRS = HEADS // 2
EPS = 1e-06
SCALE = math.log2(math.e) / math.sqrt(HDIM)
LOW = -1e30

f32 = jnp.float32
bf16 = jnp.bfloat16


def regroup(value, outer, inner, store):
    width = value.shape[-1]
    grouped = value.reshape(outer // 2, 2, inner // 2, 8, width)
    low = lax.broadcasted_iota(jnp.int32, (8, width), 0) < 4
    for a in range(inner // 2):
        evens = [grouped[c, 0, a] for c in range(outer // 2)]
        odds = [grouped[c, 1, a] for c in range(outer // 2)]
        lower = [jnp.where(low, e, pltpu.roll(o, 4, 0)) for e, o in zip(evens, odds)]
        upper = [jnp.where(low, pltpu.roll(e, 4, 0), o) for e, o in zip(evens, odds)]
        store(a * 2 * outer * 4, jnp.concatenate(lower + upper, axis=0))


def regroup_into(o_ref, value, outer, inner):
    def store(at, rows):
        o_ref[at : at + rows.shape[0], :] = rows.astype(o_ref.dtype)

    regroup(value, outer, inner, store)


def spread_kernel(half, x_ref, o_ref):
    outer, each, width = x_ref.shape
    value = x_ref[...].astype(f32).reshape(outer * each, width)
    regroup_into(o_ref, value, outer, each // UNIT)


def spread(x, half, planes, steps=1):
    rows, width = x.shape
    each = rows // planes
    outer = planes // 2
    grid_spec = pltpu.PrefetchScalarGridSpec(
        num_scalar_prefetch=1,
        grid=(steps,),
        in_specs=[pl.BlockSpec((outer, each // steps, width), lambda j, half: (half[0], j, 0))],
        out_specs=pl.BlockSpec((rows // 2 // steps, width), lambda j, half: (j, 0)),
    )
    return pl.pallas_call(
        spread_kernel,
        out_shape=jax.ShapeDtypeStruct((rows // 2, width), bf16),
        grid_spec=grid_spec,
        name="spread",
    )(half, x.reshape(planes, each, width))


def row_factor(x):
    wide = x.astype(f32)
    return lax.rsqrt(jnp.mean(wide * wide, axis=-1, keepdims=True) + EPS)


def similar(q, k):
    return lax.dot_general(q, k, (((1,), (1,)), ((), ())), preferred_element_type=f32)


def time_kernel(
    half, x_hbm, own_hbm, sent_hbm, back_own, back_sent, first_hbm, mixed_hbm, given_hbm,
    x_buf, w, w_back, mixed, first, sem, sem_w,
):
    rows, width = x_buf.shape
    tracks = rows // FRAMES
    groups = tracks // 8
    side = FRAMES * 8
    get_x = pltpu.make_async_copy(x_hbm, x_buf, sem.at[0])

    def gets(source):
        return [
            pltpu.make_async_copy(
                source.at[:, pl.ds(part * INNER + pair * PAIR, PAIR)],
                w.at[:, pl.ds(part * INNER + pair * PAIR, PAIR)],
                sem_w.at[pair * 3 + part],
            )
            for pair in range(PAIRS)
            for part in range(3)
        ]

    get_back = pltpu.make_async_copy(back_own, w_back, sem.at[2])
    get_x.start()

    @pl.when(half[0] == 0)
    def _():
        for get in gets(own_hbm):
            get.start()
        get_back.start()

    @pl.when(half[0] != 0)
    def _():
        for get in gets(sent_hbm):
            get.start()
        pltpu.make_async_copy(back_sent, w_back, sem.at[2]).start()

    same = (
        lax.broadcasted_iota(jnp.int32, (side, side), 0) % 8
        == lax.broadcasted_iota(jnp.int32, (side, side), 1) % 8
    )
    get_x.wait()
    x = x_buf[...]
    factor = row_factor(x)
    get_w = gets(own_hbm)
    for pair in range(PAIRS):
        parts = []
        for get in get_w[pair * 3 : pair * 3 + 3]:
            get.wait()
        for part in range(3):
            at = part * INNER + pair * PAIR
            y = jnp.dot(x, w[:, at : at + PAIR], preferred_element_type=f32) * factor
            parts.append(y.reshape(FRAMES, tracks, PAIR))
        places = [(head, group) for head in range(2) for group in range(groups)]
        blocks = [
            [
                y[:, group * 8 : group * 8 + 8, head * HDIM : head * HDIM + HDIM]
                .reshape(side, HDIM)
                .astype(bf16)
                for y in parts
            ]
            for head, group in places
        ]
        scores = [jnp.where(same, similar(q, k), LOW) for q, k, v in blocks]
        tops = [jnp.max(s, axis=-1, keepdims=True) for s in scores]
        es = [jnp.exp2((s - top) * SCALE) for s, top in zip(scores, tops)]
        totals = [jnp.sum(e, axis=-1, keepdims=True) for e in es]
        sums = [
            jnp.dot(e.astype(bf16), v, preferred_element_type=f32) for e, (q, k, v) in zip(es, blocks)
        ]
        for (head, group), total, summed in zip(places, totals, sums):
            at = (pair * 2 + head) * HDIM
            mixed[:, group * 8 : group * 8 + 8, at : at + HDIM] = (
                (summed * (1.0 / total)).reshape(FRAMES, 8, HDIM).astype(bf16)
            )
    m = mixed[...].reshape(rows, INNER)
    get_back.wait()
    delta = jnp.dot(m, w_back[...], preferred_element_type=f32)
    regroup_into(first, x.astype(f32) + delta, FRAMES, tracks // UNIT)

    @pl.when(half[0] == 0)
    def _():
        puts = [
            pltpu.make_async_copy(mixed, given_hbm.at[:, :, :INNER], sem.at[3]),
            pltpu.make_async_copy(first, first_hbm.at[pl.ds(0, rows), :], sem.at[4]),
        ]
        for put in puts:
            put.start()
        for put in puts:
            put.wait()

    @pl.when(half[0] != 0)
    def _():
        puts = [
            pltpu.make_async_copy(first, given_hbm.reshape(rows, width), sem.at[3]),
            pltpu.make_async_copy(mixed, mixed_hbm.at[:, pl.ds(tracks, tracks), :], sem.at[4]),
        ]
        for put in puts:
            put.start()
        for put in puts:
            put.wait()


def time_section(half, x, w_own, w_sent, back_own, back_sent):
    rows, width = x.shape
    tracks = rows // FRAMES
    hbm = pl.BlockSpec(memory_space=pl.ANY)
    return pl.pallas_call(
        time_kernel,
        out_shape=[
            jax.ShapeDtypeStruct((2 * rows, width), bf16),
            jax.ShapeDtypeStruct((FRAMES, 2 * tracks, INNER), bf16),
            jax.ShapeDtypeStruct((FRAMES, tracks, width), bf16),
        ],
        in_specs=[pl.BlockSpec(memory_space=pltpu.SMEM)] + [hbm] * 5,
        out_specs=[hbm] * 3,
        scratch_shapes=[
            pltpu.VMEM((rows, width), bf16),
            pltpu.VMEM((width, 3 * INNER), bf16),
            pltpu.VMEM((INNER, width), bf16),
            pltpu.VMEM((FRAMES, tracks, INNER), bf16),
            pltpu.VMEM((rows, width), bf16),
            pltpu.SemaphoreType.DMA((5,)),
            pltpu.SemaphoreType.DMA((3 * PAIRS,)),
        ],
        compiler_params=pltpu.CompilerParams(vmem_limit_bytes=32 << 20),
        name="time_section",
    )(half, x, w_own, w_sent, back_own, back_sent)


def join_kernel(place, columns, part_ref, whole_hbm, o_hbm, sem):
    del whole_hbm
    put = pltpu.make_async_copy(part_ref.at[columns], o_hbm.at[place], sem)
    put.start()
    put.wait()


def join(part, whole, place, columns):
    hbm = pl.BlockSpec(memory_space=pl.ANY)
    return pl.pallas_call(
        functools.partial(join_kernel, place, columns),
        out_shape=jax.ShapeDtypeStruct(whole.shape, whole.dtype),
        in_specs=[pl.BlockSpec(memory_space=pltpu.VMEM), hbm],
        out_specs=hbm,
        scratch_shapes=[pltpu.SemaphoreType.DMA],
        input_output_aliases={1: 0},
        compiler_params=pltpu.CompilerParams(vmem_limit_bytes=4 << 20),
        name="join",
    )(part, whole)


def track_kernel(
    planes, lists, m_ref, seen_ref, x_hbm, w0_hbm, wq_hbm, w1_hbm, o_ref,
    x_buf, w0, wq, w1, mixed0, first, qkv_0, qkv_1, qkv_2, mixed1, sem_more,
):
    rows = x_buf.shape[0]
    blocks = rows // BLOCK
    get_w0 = pltpu.make_async_copy(w0_hbm, w0, sem_more.at[0])
    get_x = pltpu.make_async_copy(x_hbm, x_buf, sem_more.at[1])
    get_w1 = pltpu.make_async_copy(w1_hbm, w1, sem_more.at[2])
    get_wq = pltpu.make_async_copy(wq_hbm, wq, sem_more.at[3])
    for copy in (get_w0, get_x, get_wq, get_w1):
        copy.start()
    regroup_into(mixed0, m_ref[...].astype(f32), FRAMES, planes)
    get_w0.wait()
    delta = jnp.dot(mixed0[...], w0[...], preferred_element_type=f32)
    get_x.wait()
    first[...] = (x_buf[...].astype(f32) + delta).astype(bf16)
    factor = row_factor(first[...])
    itself = lax.broadcasted_iota(jnp.int32, (BLOCK, BLOCK), 0) == lax.broadcasted_iota(
        jnp.int32, (BLOCK, BLOCK), 1
    )
    get_wq.wait()
    for pair, qkv in enumerate((qkv_0, qkv_1, qkv_2)):
        for part in range(3):
            at = part * INNER + pair * PAIR
            y = jnp.dot(first[...], wq[:, at : at + PAIR], preferred_element_type=f32) * factor
            qkv[:, part * PAIR : (part + 1) * PAIR] = y.astype(bf16)
        for head in range(2):
            at = head * HDIM
            out_at = (pair * 2 + head) * HDIM
            groups = []
            for block in range(blocks):
                others = [lists[block * 2], lists[block * 2 + 1]]
                places = [pl.ds(block * BLOCK, BLOCK)] + [
                    pl.ds(pl.multiple_of(o * BLOCK, BLOCK), BLOCK) for o in others
                ]
                allowed = [(seen_ref[block : block + 1, :] == 1) | itself] + [
                    seen_ref[pl.ds(o, 1), :] == 1 for o in others
                ]
                q = qkv[pl.ds(block * BLOCK, BLOCK), at : at + HDIM]
                groups.append((q, places, allowed))
            scores = [
                [
                    jnp.where(allow, similar(q, qkv[place, PAIR + at : PAIR + at + HDIM]), LOW)
                    for place, allow in zip(places, allowed)
                ]
                for q, places, allowed in groups
            ]
            tops = [
                jnp.max(functools.reduce(jnp.maximum, ss), axis=-1, keepdims=True) for ss in scores
            ]
            es = [[jnp.exp2((s - top) * SCALE) for s in ss] for ss, top in zip(scores, tops)]
            totals = [jnp.sum(sum(e[1:], e[0]), axis=-1, keepdims=True) for e in es]
            sums = [
                sum(
                    jnp.dot(
                        e.astype(bf16),
                        qkv[place, 2 * PAIR + at : 2 * PAIR + at + HDIM],
                        preferred_element_type=f32,
                    )
                    for e, place in zip(parts, places)
                )
                for parts, (q, places, allowed) in zip(es, groups)
            ]
            for block, (total, mixed) in enumerate(zip(totals, sums)):
                mixed1[block * BLOCK : (block + 1) * BLOCK, out_at : out_at + HDIM] = (
                    mixed * (1.0 / total)
                ).astype(bf16)
    get_w1.wait()
    delta = jnp.dot(mixed1[...], w1[...], preferred_element_type=f32)
    o_ref[...] = (first[...].astype(f32) + delta).astype(bf16)


def track_section(lists, x, mixed0, seen, w_out0, w_qkv, w_out1, planes):
    rows, width = x.shape
    vmem = pl.BlockSpec(memory_space=pltpu.VMEM)
    return pl.pallas_call(
        functools.partial(track_kernel, planes),
        out_shape=jax.ShapeDtypeStruct((rows, width), bf16),
        in_specs=[pl.BlockSpec(memory_space=pltpu.SMEM), vmem, vmem]
        + [pl.BlockSpec(memory_space=pl.ANY)] * 4,
        out_specs=vmem,
        scratch_shapes=[
            pltpu.VMEM((rows, width), bf16),
            pltpu.VMEM((INNER, width), bf16),
            pltpu.VMEM((width, 3 * INNER), bf16),
            pltpu.VMEM((INNER, width), bf16),
            pltpu.VMEM((rows, INNER), bf16),
            pltpu.VMEM((rows, width), bf16),
            pltpu.VMEM((rows, 3 * PAIR), bf16),
            pltpu.VMEM((rows, 3 * PAIR), bf16),
            pltpu.VMEM((rows, 3 * PAIR), bf16),
            pltpu.VMEM((rows, INNER), bf16),
            pltpu.SemaphoreType.DMA((4,)),
        ],
        compiler_params=pltpu.CompilerParams(vmem_limit_bytes=40 << 20),
        name="track_section",
    )(lists, mixed0, seen, x, w_out0, w_qkv, w_out1)


def exchange(value, axis):
    return lax.all_to_all(value, axis, split_axis=0, concat_axis=0, tiled=True)


def on_device(tracks_in, w_qkv, w_out, visible, neighbours):
    segment_no = lax.axis_index("segment")
    video_no = lax.axis_index("z")
    planes = lax.axis_size("z")
    frames = lax.axis_size("plane")
    x = tracks_in[0, 0]
    rows, width = x.shape
    per_chip = rows // frames
    w_in, w_back = w_qkv[0], w_out[0]
    seen = visible[0, 0].reshape(rows // BLOCK, BLOCK)
    lists = lax.dynamic_index_in_dim(neighbours[0], video_no, 0, keepdims=False).reshape(-1)
    half = segment_no.reshape(1).astype(jnp.int32)
    sent = spread(x, half, planes).reshape(frames, per_chip // 2, width)
    sent, w_in_sent, w_back_sent = lax.optimization_barrier((sent, w_in, w_back))
    moved = exchange(sent, "plane").reshape(rows // 2, width)
    w_in_first = lax.ppermute(w_in_sent, "segment", [(0, 1)])
    w_back_first = lax.ppermute(w_back_sent, "segment", [(0, 1)])
    first, mixed0, given = time_section(half, moved, w_in, w_in_first, w_back, w_back_first)
    taken = lax.ppermute(given, "segment", [(0, 1), (1, 0)])
    each = per_chip // 2

    def track_order():
        other = taken.reshape(rows // 2, width)
        whole = join(other, first, (pl.ds(rows // 2, rows // 2),), (pl.ds(0, rows // 2),))
        return exchange(whole.reshape(planes, -1, width), "z").reshape(rows, width)

    def section_two():
        everything = slice(None)
        place = (everything, pl.ds(0, each), everything)
        whole = join(taken, mixed0, place, (everything, everything, pl.ds(0, INNER)))
        back = exchange(whole, "plane").reshape(rows, INNER)
        return track_section(lists, x, back, seen, w_back_first, w_in, w_back, planes)

    result = lax.cond(segment_no == 0, track_order, section_two)
    return result[None, None, None]


def solution(mesh):
    frames = FRAMES
    devices = mesh.devices.reshape(mesh.devices.shape[0], -1, frames)
    grid = Mesh(devices, ("segment", "z", "plane"))
    seq = ("z", "plane")
    return jax.shard_map(
        on_device,
        mesh=grid,
        in_specs=(
            P(None, seq, None, None),
            P("segment", None, None),
            P("segment", None, None),
            P(None, seq, None),
            P(),
        ),
        out_specs=P("segment", None, seq, None, None),
        check_vma=False,
    )
```

time: 94.8 us -> 71.9 us (0.76)
  the two profiles are of different devices: /device:TPU:1 before, /device:TPU:8 now
where the time goes in v1:
time: 71.9 us; the launch traced here: 71.5 us
  blocking collectives  51.9 us (72%)
  Pallas kernels  12.3 us (17%)
  starting transfers between devices  3.72 us (5%)
  waiting for transfers between devices  2.4 us (3%)
  local copies, waits for them, and re-layouts  1.16 us (2%)
    all_to_all x2, blocking collectives, exchange(): return lax.all_to_all(value, axis, split_axis=0, concat_axis=0, tiled=True)  51.9 us
    pallas_call x1, Pallas kernels, time_section(): pl.pallas_call(time_kernel, out_shape=[jax.ShapeDtypeStruct((2 * rows, wi...  7.87 us
    ppermute x1, waiting for transfers between devices, on_device(): taken = lax.ppermute(given, 'segment', [(0, 1), (1, 0)])  2.39 us
    pallas_call x1, Pallas kernels, spread(): pl.pallas_call(spread_kernel, out_shape=jax.ShapeDtypeStruct((rows // 2,...  2.36 us
    ppermute x1, starting transfers between devices, on_device(): w_in_first = lax.ppermute(w_in_sent, 'segment', [(0, 1)])  2.18 us
    pallas_call x1, Pallas kernels, join(): pl.pallas_call(functools.partial(join_kernel, place, columns), out_shape=...  2.02 us
    ppermute x1, starting transfers between devices, on_device(): w_back_first = lax.ppermute(w_back_sent, 'segment', [(0, 1)])  1.44 us
  transfers between devices with their start and end apart: 3, of which 1 were waited for; matrix products, arithmetic and copies ran while one was open for 0% of the time, Pallas kernels for 0%

profile of v1, /device:TPU:8, one launch (start us, length us, event | category | flops | bytes accessed | tf_op | source)
XLA Modules:
  0.0 71.5 jit_solution(4847117767653610456)
XLA Ops:
  0.0 0.0 copy-start
  0.0 2.4 %spread.1 = bf16[256,1536]{1,0:T(8,128)(2,1)} custom-call(s32[1]{0:T(128)} %bitcast.7.half, bf16[8,64,1536]{2,1,0:T(8,128)(2,1)} %bitcast.21), custom_call_target="tpu_custom_call" | custom-call | tf_op jit(solution)/shard_map/spread/pallas_call | solution.py:62
  2.4 2.2 %collective-permute-start = (bf16[1536,2304]{1,0:T(8,128)(2,1)}, bf16[1536,2304]{1,0:T(8,128)(2,1)S(1)}, u32[]{:S(2)}, u32[]{:S(2)}) collective-permute-start(bf16[1536,2304]{1,0:T(8,128)(2,1)} %bitcast.15), channel_id=1, source_target_pairs={{0,128},{1,129},{2,130},{3,131},{4,132},{5,133},{6,134},{7,135},{8... | collective-permute-start | bytes 21233672 | tf_op jit(solution)/shard_map/ppermute | solution.py:348
  4.6 0.0 copy-done
  4.6 1.4 %collective-permute-start.1 = (bf16[768,1536]{1,0:T(8,128)(2,1)S(1)}, bf16[768,1536]{1,0:T(8,128)(2,1)S(1)}, u32[]{:S(2)}, u32[]{:S(2)}) collective-permute-start(bf16[768,1536]{1,0:T(8,128)(2,1)S(1)} %bitcast.18), channel_id=1, source_target_pairs={{0,128},{1,129},{2,130},{3,131},{4,132},{5,133},{6,134},{7,135},{8... | collective-permute-start | bytes 7077896 | tf_op jit(solution)/shard_map/ppermute | solution.py:349
  6.0 18.9 %all_to_all.14 = bf16[16,16,1536]{2,1,0:T(8,128)(2,1)S(1)} all-to-all(bf16[16,16,1536]{2,1,0:T(8,128)(2,1)} %bitcast.26), channel_id=1, replica_groups=mesh['segment'=2,'z'=8,'plane'=16] {'plane'}, dimensions={0} | all-to-all | bytes 1572864 | tf_op jit(solution)/shard_map/all_to_all | solution.py:330
  24.9 0.0 collective-permute-done.1.back_sent
  24.9 0.0 copy-start.1
  24.9 0.0 collective-permute-done.sent_hbm
  25.0 0.0 copy-start.2
  25.0 0.0 copy-start.3
  25.0 7.9 %time_section.1 = (bf16[512,1536]{1,0:T(8,128)(2,1)}, bf16[16,32,768]{2,1,0:T(8,128)(2,1)}, bf16[16,16,1536]{2,1,0:T(8,128)(2,1)S(1)}) custom-call(s32[1]{0:T(128)} %bitcast.7.half, bf16[256,1536]{1,0:T(8,128)(2,1)S(1)} %bitcast.14, bf16[1536,2304]{1,0:T(8,128)(2,1)} %bitcast.16, bf16[1536,2304]{1,0:T(8,128)(2,1)S(1)} %collective-permute-done.sent_hbm, ...), custom_call_target="tpu_custom_call" | custom-call | tf_op jit(solution)/shard_map/time_section/pallas_call | solution.py:185
  32.9 0.0 copy-done.1
  32.9 0.1 collective-permute-start.2
  33.0 2.4 %collective-permute-done.2 = bf16[16,16,1536]{2,1,0:T(8,128)(2,1)} collective-permute-done((bf16[16,16,1536]{2,1,0:T(8,128)(2,1)S(1)}, bf16[16,16,1536]{2,1,0:T(8,128)(2,1)}, u32[]{:S(2)}, u32[]{:S(2)}) %collective-permute-start.2) | collective-permute-done | bytes 786464 | tf_op jit(solution)/shard_map/ppermute | solution.py:351
  35.4 0.0 copy-done.2
  35.4 0.0 copy-done.3
  35.4 35.0 %conditional.1 = (bf16[1,1,1,512,1536]{4,3,2,1,0:T(8,128)(2,1)S(1)}) conditional(s32[]{:T(128)} %convert_element_type.3, (s32[]{:T(128)}, s32[1,8,4,2]{1,3,2,0:T(2,128)S(1)}, bf16[16,16,1536]{2,1,0:T(8,128)(2,1)}, bf16[16,32,768]{2,1,0:T(8,128)(2,1)}, s32[1,1,512]{2,1,0:T(1,128)S(1)}, /*index=5*/bf16[1,1,512,1536]{3,2,1,0:T(8,128)(2,1)}, ...), branch_computations={%region_0.1_spmd, %region_1.2_spmd} | conditional | flops 3 | bytes 3145736 | solution.py:366
  35.4 2.0 %join.3 = bf16[512,1536]{1,0:T(8,128)(2,1)} custom-call(bf16[256,1536]{1,0:T(8,128)(2,1)} %bitcast.4.part_ref, bf16[512,1536]{1,0:T(8,128)(2,1)} %get-tuple-element.53.whole_hbm), custom_call_target="tpu_custom_call", output_to_operand_aliasing={{}: (1, {})} | custom-call | tf_op jit(solution)/shard_map/cond/branch_1_fun/join/pallas_call | solution.py:217
  37.4 33.0 %all_to_all.13 = bf16[8,64,1536]{2,1,0:T(8,128)(2,1)S(1)} all-to-all(bf16[8,64,1536]{2,1,0:T(8,128)(2,1)} %bitcast.25), channel_id=1, replica_groups=mesh['segment'=2,'z'=8,'plane'=16] {'z'}, dimensions={0} | all-to-all | bytes 3145728 | tf_op jit(solution)/shard_map/cond/branch_1_fun/all_to_all | solution.py:330
  70.4 1.1 %copy.19 = bf16[1,1,1,512,1536]{4,3,2,1,0:T(8,128)(2,1)} copy(bf16[1,1,1,512,1536]{4,3,2,1,0:T(8,128)(2,1)S(1)} %get-tuple-element.66) | data formatting | bytes 3145728
Async XLA Ops:
  0.0 4.6 %copy-start = (bf16[1,768,1536]{2,1,0:T(8,128)(2,1)S(1)}, bf16[1,768,1536]{2,1,0:T(8,128)(2,1)}, u32[]{:S(2)}) copy-start(bf16[1,768,1536]{2,1,0:T(8,128)(2,1)} %param.9) | copy-start | bytes 7077892
  2.4 22.6 %collective-permute-start = (bf16[1536,2304]{1,0:T(8,128)(2,1)}, bf16[1536,2304]{1,0:T(8,128)(2,1)S(1)}, u32[]{:S(2)}, u32[]{:S(2)}) collective-permute-start(bf16[1536,2304]{1,0:T(8,128)(2,1)} %bitcast.15), channel_id=1, source_target_pairs={{0,128},{1,129},{2,130},{3,131},{4,132},{5,133},{6,134},{7,135},{8... | collective-permute-start | bytes 21233672 | tf_op jit(solution)/shard_map/ppermute | solution.py:348
  4.6 20.4 %collective-permute-start.1 = (bf16[768,1536]{1,0:T(8,128)(2,1)S(1)}, bf16[768,1536]{1,0:T(8,128)(2,1)S(1)}, u32[]{:S(2)}, u32[]{:S(2)}) collective-permute-start(bf16[768,1536]{1,0:T(8,128)(2,1)S(1)} %bitcast.18), channel_id=1, source_target_pairs={{0,128},{1,129},{2,130},{3,131},{4,132},{5,133},{6,134},{7,135},{8... | collective-permute-start | bytes 7077896 | tf_op jit(solution)/shard_map/ppermute | solution.py:349
  24.9 7.9 %copy-start.1 = (bf16[768,1536]{1,0:T(8,128)(2,1)}, bf16[768,1536]{1,0:T(8,128)(2,1)S(1)}, u32[]{:S(2)}) copy-start(bf16[768,1536]{1,0:T(8,128)(2,1)S(1)} %collective-permute-done.1.back_sent) | copy-start | bytes 7077892
  25.0 10.4 %copy-start.2 = (s32[1,8,4,2]{1,3,2,0:T(2,128)S(1)}, s32[1,8,4,2]{1,3,2,0:T(2,128)}, u32[]{:S(2)}) copy-start(s32[1,8,4,2]{1,3,2,0:T(2,128)} %param.11) | copy-start | bytes 772
  25.0 10.4 %copy-start.3 = (s32[1,1,512]{2,1,0:T(1,128)S(1)}, s32[1,1,512]{2,1,0:T(1,128)}, u32[]{:S(2)}) copy-start(s32[1,1,512]{2,1,0:T(1,128)} %param.10) | copy-start | bytes 6148
  32.9 2.5 %collective-permute-start.2 = (bf16[16,16,1536]{2,1,0:T(8,128)(2,1)S(1)}, bf16[16,16,1536]{2,1,0:T(8,128)(2,1)}, u32[]{:S(2)}, u32[]{:S(2)}) collective-permute-start(bf16[16,16,1536]{2,1,0:T(8,128)(2,1)S(1)} %get-tuple-element.63), channel_id=1, source_target_pairs={{0,128},{128,0},{1,129},{129,1},{2,130},{130,2},{3,131},{131,3},{4... | collective-permute-start | bytes 2359304 | tf_op jit(solution)/shard_map/ppermute | solution.py:351

commit v2 on v1

--- a/solution.py
+++ b/solution.py
@@ -76,50 +76,48 @@
     return lax.dot_general(q, k, (((1,), (1,)), ((), ())), preferred_element_type=f32)
 
 
+def qkv_copies(source, target, sem):
+    copies = []
+    for pair in range(PAIRS):
+        for part in range(3):
+            columns = pl.ds(part * INNER + pair * PAIR, PAIR)
+            copies.append(
+                pltpu.make_async_copy(
+                    source.at[:, columns], target.at[:, columns], sem.at[pair * 3 + part]
+                )
+            )
+    return copies
+
+
 def time_kernel(
-    half, x_hbm, own_hbm, sent_hbm, back_own, back_sent, first_hbm, mixed_hbm, given_hbm,
-    x_buf, w, w_back, mixed, first, sem, sem_w,
+    half, x_buf, own_hbm, sent_hbm, back_own, back_sent, first_ref, mixed_hbm, given_ref,
+    w, w_back, mixed, sem, sem_w, sem_out,
 ):
     rows, width = x_buf.shape
     tracks = rows // FRAMES
     groups = tracks // 8
     side = FRAMES * 8
-    get_x = pltpu.make_async_copy(x_hbm, x_buf, sem.at[0])
-
-    def gets(source):
-        return [
-            pltpu.make_async_copy(
-                source.at[:, pl.ds(part * INNER + pair * PAIR, PAIR)],
-                w.at[:, pl.ds(part * INNER + pair * PAIR, PAIR)],
-                sem_w.at[pair * 3 + part],
-            )
-            for pair in range(PAIRS)
-            for part in range(3)
-        ]
-
-    get_back = pltpu.make_async_copy(back_own, w_back, sem.at[2])
-    get_x.start()
+    get_back = pltpu.make_async_copy(back_own, w_back, sem)
 
     @pl.when(half[0] == 0)
     def _():
-        for get in gets(own_hbm):
+        for get in qkv_copies(own_hbm, w, sem_w):
             get.start()
         get_back.start()
 
     @pl.when(half[0] != 0)
     def _():
-        for get in gets(sent_hbm):
+        for get in qkv_copies(sent_hbm, w, sem_w):
             get.start()
-        pltpu.make_async_copy(back_sent, w_back, sem.at[2]).start()
+        pltpu.make_async_copy(back_sent, w_back, sem).start()
 
     same = (
         lax.broadcasted_iota(jnp.int32, (side, side), 0) % 8
         == lax.broadcasted_iota(jnp.int32, (side, side), 1) % 8
     )
-    get_x.wait()
     x = x_buf[...]
     factor = row_factor(x)
-    get_w = gets(own_hbm)
+    get_w = qkv_copies(own_hbm, w, sem_w)
     for pair in range(PAIRS):
         parts = []
         for get in get_w[pair * 3 : pair * 3 + 3]:
@@ -153,77 +151,89 @@
     m = mixed[...].reshape(rows, INNER)
     get_back.wait()
     delta = jnp.dot(m, w_back[...], preferred_element_type=f32)
-    regroup_into(first, x.astype(f32) + delta, FRAMES, tracks // UNIT)
+    first = x.astype(f32) + delta
 
     @pl.when(half[0] == 0)
     def _():
-        puts = [
-            pltpu.make_async_copy(mixed, given_hbm.at[:, :, :INNER], sem.at[3]),
-            pltpu.make_async_copy(first, first_hbm.at[pl.ds(0, rows), :], sem.at[4]),
-        ]
-        for put in puts:
-            put.start()
-        for put in puts:
-            put.wait()
+        given_ref[:, :, :INNER] = mixed[...]
+        regroup_into(first_ref.at[pl.ds(0, rows), :], first, FRAMES, tracks // UNIT)
 
     @pl.when(half[0] != 0)
     def _():
-        puts = [
-            pltpu.make_async_copy(first, given_hbm.reshape(rows, width), sem.at[3]),
-            pltpu.make_async_copy(mixed, mixed_hbm.at[:, pl.ds(tracks, tracks), :], sem.at[4]),
-        ]
-        for put in puts:
-            put.start()
-        for put in puts:
-            put.wait()
+        put = pltpu.make_async_copy(mixed, mixed_hbm.at[:, pl.ds(tracks, tracks), :], sem_out)
+        put.start()
+        regroup_into(given_ref.reshape(rows, width), first, FRAMES, tracks // UNIT)
+        put.wait()
 
 
 def time_section(half, x, w_own, w_sent, back_own, back_sent):
     rows, width = x.shape
     tracks = rows // FRAMES
+    vmem = pl.BlockSpec(memory_space=pltpu.VMEM)
     hbm = pl.BlockSpec(memory_space=pl.ANY)
     return pl.pallas_call(
         time_kernel,
         out_shape=[
-            jax.ShapeDtypeStruct((2 * rows, width), bf16),
+            pltpu.VMEM((2 * rows, width), bf16),
             jax.ShapeDtypeStruct((FRAMES, 2 * tracks, INNER), bf16),
-            jax.ShapeDtypeStruct((FRAMES, tracks, width), bf16),
-        ],
-        in_specs=[pl.BlockSpec(memory_space=pltpu.SMEM)] + [hbm] * 5,
-        out_specs=[hbm] * 3,
+            pltpu.VMEM((FRAMES, tracks, width), bf16),
+        ],
+        in_specs=[
+            pl.BlockSpec(memory_space=pltpu.SMEM),
+            vmem,
+            pl.BlockSpec(memory_space=pltpu.HBM),
+            hbm,
+            pl.BlockSpec(memory_space=pltpu.HBM),
+            hbm,
+        ],
+        out_specs=[vmem, hbm, vmem],
         scratch_shapes=[
-            pltpu.VMEM((rows, width), bf16),
             pltpu.VMEM((width, 3 * INNER), bf16),
             pltpu.VMEM((INNER, width), bf16),
             pltpu.VMEM((FRAMES, tracks, INNER), bf16),
-            pltpu.VMEM((rows, width), bf16),
-            pltpu.SemaphoreType.DMA((5,)),
+            pltpu.SemaphoreType.DMA,
             pltpu.SemaphoreType.DMA((3 * PAIRS,)),
-        ],
-        compiler_params=pltpu.CompilerParams(vmem_limit_bytes=32 << 20),
+            pltpu.SemaphoreType.DMA,
+        ],
+        compiler_params=pltpu.CompilerParams(vmem_limit_bytes=20 << 20),
         name="time_section",
     )(half, x, w_own, w_sent, back_own, back_sent)
 
 
-def join_kernel(place, columns, part_ref, whole_hbm, o_hbm, sem):
-    del whole_hbm
-    put = pltpu.make_async_copy(part_ref.at[columns], o_hbm.at[place], sem)
-    put.start()
-    put.wait()
-
-
-def join(part, whole, place, columns):
+def join_kernel(half, part_ref, first_in, mixed_in, first_out, mixed_out, sem):
+    del first_in, mixed_in
+    frames, tracks, width = part_ref.shape
+    rows = frames * tracks
+
+    @pl.when(half[0] == 0)
+    def _():
+        first_out[rows:, :] = part_ref[...].reshape(rows, width)
+
+    @pl.when(half[0] != 0)
+    def _():
+        put = pltpu.make_async_copy(
+            part_ref.at[:, :, pl.ds(0, INNER)], mixed_out.at[:, pl.ds(0, tracks), :], sem
+        )
+        put.start()
+        put.wait()
+
+
+def join(half, part, first, mixed):
+    vmem = pl.BlockSpec(memory_space=pltpu.VMEM)
     hbm = pl.BlockSpec(memory_space=pl.ANY)
     return pl.pallas_call(
-        functools.partial(join_kernel, place, columns),
-        out_shape=jax.ShapeDtypeStruct(whole.shape, whole.dtype),
-        in_specs=[pl.BlockSpec(memory_space=pltpu.VMEM), hbm],
-        out_specs=hbm,
+        join_kernel,
+        out_shape=[
+            pltpu.VMEM(first.shape, first.dtype),
+            jax.ShapeDtypeStruct(mixed.shape, mixed.dtype),
+        ],
+        in_specs=[pl.BlockSpec(memory_space=pltpu.SMEM), vmem, vmem, hbm],
+        out_specs=[vmem, hbm],
         scratch_shapes=[pltpu.SemaphoreType.DMA],
-        input_output_aliases={1: 0},
+        input_output_aliases={2: 0, 3: 1},
         compiler_params=pltpu.CompilerParams(vmem_limit_bytes=4 << 20),
         name="join",
-    )(part, whole)
+    )(half, part, first, mixed)
 
 
 def track_kernel(
@@ -306,7 +316,7 @@
         functools.partial(track_kernel, planes),
         out_shape=jax.ShapeDtypeStruct((rows, width), bf16),
         in_specs=[pl.BlockSpec(memory_space=pltpu.SMEM), vmem, vmem]
-        + [pl.BlockSpec(memory_space=pl.ANY)] * 4,
+        + [pl.BlockSpec(memory_space=pltpu.HBM)] * 4,
         out_specs=vmem,
         scratch_shapes=[
             pltpu.VMEM((rows, width), bf16),
@@ -349,18 +359,13 @@
     w_back_first = lax.ppermute(w_back_sent, "segment", [(0, 1)])
     first, mixed0, given = time_section(half, moved, w_in, w_in_first, w_back, w_back_first)
     taken = lax.ppermute(given, "segment", [(0, 1), (1, 0)])
-    each = per_chip // 2
+    first, mixed0 = join(half, taken, first, mixed0)
 
     def track_order():
-        other = taken.reshape(rows // 2, width)
-        whole = join(other, first, (pl.ds(rows // 2, rows // 2),), (pl.ds(0, rows // 2),))
-        return exchange(whole.reshape(planes, -1, width), "z").reshape(rows, width)
+        return exchange(first.reshape(planes, -1, width), "z").reshape(rows, width)
 
     def section_two():
-        everything = slice(None)
-        place = (everything, pl.ds(0, each), everything)
-        whole = join(taken, mixed0, place, (everything, everything, pl.ds(0, INNER)))
-        back = exchange(whole, "plane").reshape(rows, INNER)
+        back = exchange(mixed0, "plane").reshape(rows, INNER)
         return track_section(lists, x, back, seen, w_back_first, w_in, w_back, planes)
 
     result = lax.cond(segment_no == 0, track_order, section_two)

time: 71.9 us -> 69.2 us (0.962)
  Pallas kernels: 12.3 us -> 9.36 us
    pallas_call x2, Pallas kernels: 9.89 us -> 7.15 us  [the longest x1 7.08 us: time_section(): pl.pallas_call(time_kernel, out_shape=[pltpu.VMEM((2 * rows, width), bf16...]
    unnamed x9 -> x7, local copies, waits for them, and re-layouts: 1.16 us -> 1.77 us
where the time goes in v2:
time: 69.2 us; the launch traced here: 68.9 us
  blocking collectives  51.7 us (75%)
  Pallas kernels  9.36 us (14%)
  starting transfers between devices  3.72 us (5%)
  waiting for transfers between devices  2.27 us (3%)
  local copies, waits for them, and re-layouts  1.77 us (3%)
    all_to_all x2, blocking collectives, exchange(): return lax.all_to_all(value, axis, split_axis=0, concat_axis=0, tiled=True)  51.7 us
    pallas_call x1, Pallas kernels, time_section(): pl.pallas_call(time_kernel, out_shape=[pltpu.VMEM((2 * rows, width), bf16...  7.08 us
    ppermute x1, waiting for transfers between devices, on_device(): taken = lax.ppermute(given, 'segment', [(0, 1), (1, 0)])  2.26 us
    pallas_call x1, Pallas kernels, spread(): pl.pallas_call(spread_kernel, out_shape=jax.ShapeDtypeStruct((rows // 2,...  2.21 us
    ppermute x1, starting transfers between devices, on_device(): w_in_first = lax.ppermute(w_in_sent, 'segment', [(0, 1)])  2.18 us
    unnamed x7, local copies, waits for them, and re-layouts  1.77 us
    ppermute x1, starting transfers between devices, on_device(): w_back_first = lax.ppermute(w_back_sent, 'segment', [(0, 1)])  1.44 us
  transfers between devices with their start and end apart: 3, of which 1 were waited for; matrix products, arithmetic and copies ran while one was open for 0% of the time, Pallas kernels for 0%

profile of v2, /device:TPU:8, one launch (start us, length us, event | category | flops | bytes accessed | tf_op | source)
XLA Modules:
  0.0 68.9 jit_solution(14907111715550051039)
XLA Ops:
  0.0 2.2 %spread.1 = bf16[256,1536]{1,0:T(8,128)(2,1)} custom-call(s32[1]{0:T(128)} %bitcast.6.half, bf16[8,64,1536]{2,1,0:T(8,128)(2,1)} %bitcast.18), custom_call_target="tpu_custom_call" | custom-call | tf_op jit(solution)/shard_map/spread/pallas_call | solution.py:62
  2.2 2.2 %collective-permute-start = (bf16[1536,2304]{1,0:T(8,128)(2,1)}, bf16[1536,2304]{1,0:T(8,128)(2,1)S(1)}, u32[]{:S(2)}, u32[]{:S(2)}) collective-permute-start(bf16[1536,2304]{1,0:T(8,128)(2,1)} %bitcast.15), channel_id=1, source_target_pairs={{0,128},{1,129},{2,130},{3,131},{4,132},{5,133},{6,134},{7,135},{8... | collective-permute-start | bytes 21233672 | tf_op jit(solution)/shard_map/ppermute | solution.py:358
  4.4 1.4 %collective-permute-start.1 = (bf16[768,1536]{1,0:T(8,128)(2,1)}, bf16[768,1536]{1,0:T(8,128)(2,1)S(1)}, u32[]{:S(2)}, u32[]{:S(2)}) collective-permute-start(bf16[768,1536]{1,0:T(8,128)(2,1)} %bitcast.10.back_own), channel_id=1, source_target_pairs={{0,128},{1,129},{2,130},{3,131},{4,132},{5,133},{6,134},{7,135},{8... | collective-permute-start | bytes 7077896 | tf_op jit(solution)/shard_map/ppermute | solution.py:359
  5.9 18.9 %all_to_all.14 = bf16[16,16,1536]{2,1,0:T(8,128)(2,1)S(1)} all-to-all(bf16[16,16,1536]{2,1,0:T(8,128)(2,1)} %bitcast.22), channel_id=1, replica_groups=mesh['segment'=2,'z'=8,'plane'=16] {'plane'}, dimensions={0} | all-to-all | bytes 1572864 | tf_op jit(solution)/shard_map/all_to_all | solution.py:340
  24.8 0.0 collective-permute-done.1.back_sent
  24.8 0.0 copy-start
  24.8 0.0 collective-permute-done.sent_hbm
  24.8 7.1 %time_section.1 = (bf16[512,1536]{1,0:T(8,128)(2,1)S(1)}, bf16[16,32,768]{2,1,0:T(8,128)(2,1)}, bf16[16,16,1536]{2,1,0:T(8,128)(2,1)S(1)}) custom-call(s32[1]{0:T(128)} %bitcast.6.half, bf16[256,1536]{1,0:T(8,128)(2,1)S(1)} %bitcast.14, bf16[1536,2304]{1,0:T(8,128)(2,1)} %bitcast.16, bf16[1536,2304]{1,0:T(8,128)(2,1)S(1)} %collective-permute-done.sent_hbm, ...), custom_call_target="tpu_custom_call" | custom-call | tf_op jit(solution)/shard_map/time_section/pallas_call | solution.py:174
  31.9 0.0 copy-done
  31.9 0.1 collective-permute-start.2
  32.0 2.3 %collective-permute-done.2.part_ref = bf16[16,16,1536]{2,1,0:T(8,128)(2,1)S(1)} collective-permute-done((bf16[16,16,1536]{2,1,0:T(8,128)(2,1)S(1)}, bf16[16,16,1536]{2,1,0:T(8,128)(2,1)S(1)}, u32[]{:S(2)}, u32[]{:S(2)}) %collective-permute-start.2) | collective-permute-done | bytes 786464 | tf_op jit(solution)/shard_map/ppermute | solution.py:361
  34.3 0.0 copy-start.2
  34.3 0.0 copy-start.3
  34.3 0.1 join.1
  34.3 0.6 copy-done.2
  35.0 0.0 copy-done.3
  35.0 32.8 %conditional.1 = (bf16[1,1,1,512,1536]{4,3,2,1,0:T(8,128)(2,1)S(1)}) conditional(s32[]{:T(128)} %convert_element_type.3, (s32[]{:T(128)}, s32[1,8,4,2]{1,3,2,0:T(2,128)S(1)}, bf16[16,32,768]{2,1,0:T(8,128)(2,1)}, s32[1,1,512]{2,1,0:T(1,128)S(1)}, bf16[1,1,512,1536]{3,2,1,0:T(8,128)(2,1)}, /*index=5*/bf16[768,1536]{1,0:T(8,128)(2,1)}, ...), branch_computations={%region_0.1_spmd, %region_1.2_spmd} | conditional | flops 3 | bytes 8651498 | solution.py:371
  35.0 32.8 %all_to_all.13 = bf16[8,64,1536]{2,1,0:T(8,128)(2,1)S(1)} all-to-all(bf16[8,64,1536]{2,1,0:T(8,128)(2,1)S(1)} %bitcast.12), channel_id=1, replica_groups=mesh['segment'=2,'z'=8,'plane'=16] {'z'}, dimensions={0} | all-to-all | bytes 3145728 | tf_op jit(solution)/shard_map/cond/branch_1_fun/all_to_all | solution.py:340
  67.7 1.1 %copy.19 = bf16[1,1,1,512,1536]{4,3,2,1,0:T(8,128)(2,1)} copy(bf16[1,1,1,512,1536]{4,3,2,1,0:T(8,128)(2,1)S(1)} %get-tuple-element.62) | data formatting | bytes 3145728
Async XLA Ops:
  2.2 22.6 %collective-permute-start = (bf16[1536,2304]{1,0:T(8,128)(2,1)}, bf16[1536,2304]{1,0:T(8,128)(2,1)S(1)}, u32[]{:S(2)}, u32[]{:S(2)}) collective-permute-start(bf16[1536,2304]{1,0:T(8,128)(2,1)} %bitcast.15), channel_id=1, source_target_pairs={{0,128},{1,129},{2,130},{3,131},{4,132},{5,133},{6,134},{7,135},{8... | collective-permute-start | bytes 21233672 | tf_op jit(solution)/shard_map/ppermute | solution.py:358
  4.4 20.4 %collective-permute-start.1 = (bf16[768,1536]{1,0:T(8,128)(2,1)}, bf16[768,1536]{1,0:T(8,128)(2,1)S(1)}, u32[]{:S(2)}, u32[]{:S(2)}) collective-permute-start(bf16[768,1536]{1,0:T(8,128)(2,1)} %bitcast.10.back_own), channel_id=1, source_target_pairs={{0,128},{1,129},{2,130},{3,131},{4,132},{5,133},{6,134},{7,135},{8... | collective-permute-start | bytes 7077896 | tf_op jit(solution)/shard_map/ppermute | solution.py:359
  24.8 7.1 %copy-start = (bf16[768,1536]{1,0:T(8,128)(2,1)}, bf16[768,1536]{1,0:T(8,128)(2,1)S(1)}, u32[]{:S(2)}) copy-start(bf16[768,1536]{1,0:T(8,128)(2,1)S(1)} %collective-permute-done.1.back_sent) | copy-start | bytes 7077892
  31.9 2.4 %collective-permute-start.2 = (bf16[16,16,1536]{2,1,0:T(8,128)(2,1)S(1)}, bf16[16,16,1536]{2,1,0:T(8,128)(2,1)S(1)}, u32[]{:S(2)}, u32[]{:S(2)}) collective-permute-start(bf16[16,16,1536]{2,1,0:T(8,128)(2,1)S(1)} %get-tuple-element.57), channel_id=1, source_target_pairs={{0,128},{128,0},{1,129},{129,1},{2,130},{130,2},{3,131},{131,3},{4... | collective-permute-start | bytes 2359304 | tf_op jit(solution)/shard_map/ppermute | solution.py:361
  34.3 0.7 copy-start.2
  34.3 0.7 %copy-start.3 = (s32[1,1,512]{2,1,0:T(1,128)S(1)}, s32[1,1,512]{2,1,0:T(1,128)}, u32[]{:S(2)}) copy-start(s32[1,1,512]{2,1,0:T(1,128)} %param.10) | copy-start | bytes 6148

commit v3 on v2

--- a/solution.py
+++ b/solution.py
@@ -43,26 +43,44 @@
     regroup(value, outer, inner, store)
 
 
-def spread_kernel(half, x_ref, o_ref):
-    outer, each, width = x_ref.shape
-    value = x_ref[...].astype(f32).reshape(outer * each, width)
-    regroup_into(o_ref, value, outer, each // UNIT)
-
-
-def spread(x, half, planes, steps=1):
+def spread_kernel(planes, half, x_hbm, o_ref, x_buf, sem):
+    outer, each, width = x_buf.shape
+    pieces = sem.shape[0]
+    step = each // pieces
+    gets = []
+    for piece in range(pieces):
+        part = pl.ds(piece * step, step)
+        gets.append(
+            pltpu.make_async_copy(
+                x_hbm.at[pl.ds(half[0] * outer, outer), part, :], x_buf.at[:, part, :], sem.at[piece]
+            )
+        )
+    for get in gets:
+        get.start()
+    for piece, get in enumerate(gets):
+        get.wait()
+        value = x_buf[:, piece * step : (piece + 1) * step, :].astype(f32)
+        regroup_into(
+            o_ref.at[pl.ds(piece * outer * step, outer * step), :],
+            value.reshape(outer * step, width),
+            outer,
+            step // UNIT,
+        )
+
+
+def spread(x, half, planes, pieces=4):
     rows, width = x.shape
     each = rows // planes
-    outer = planes // 2
-    grid_spec = pltpu.PrefetchScalarGridSpec(
-        num_scalar_prefetch=1,
-        grid=(steps,),
-        in_specs=[pl.BlockSpec((outer, each // steps, width), lambda j, half: (half[0], j, 0))],
-        out_specs=pl.BlockSpec((rows // 2 // steps, width), lambda j, half: (j, 0)),
-    )
     return pl.pallas_call(
-        spread_kernel,
-        out_shape=jax.ShapeDtypeStruct((rows // 2, width), bf16),
-        grid_spec=grid_spec,
+        functools.partial(spread_kernel, planes),
+        out_shape=pltpu.VMEM((rows // 2, width), bf16),
+        in_specs=[pl.BlockSpec(memory_space=pltpu.SMEM), pl.BlockSpec(memory_space=pl.ANY)],
+        out_specs=pl.BlockSpec(memory_space=pltpu.VMEM),
+        scratch_shapes=[
+            pltpu.VMEM((planes // 2, each, width), bf16),
+            pltpu.SemaphoreType.DMA((pieces,)),
+        ],
+        compiler_params=pltpu.CompilerParams(vmem_limit_bytes=8 << 20),
         name="spread",
     )(half, x.reshape(planes, each, width))
 

time: 69.2 us -> 68.1 us (0.984)
  Pallas kernels: 9.36 us -> 8.46 us
    pallas_call x1, Pallas kernels: 2.21 us -> 1.3 us  [spread(): pl.pallas_call(functools.partial(spread_kernel, planes), out_shape=pltpu....]
where the time goes in v3:
time: 68.1 us; the launch traced here: 67.8 us
  blocking collectives  51.5 us (76%)
  Pallas kernels  8.46 us (12%)
  starting transfers between devices  3.73 us (5%)
  waiting for transfers between devices  2.27 us (3%)
  local copies, waits for them, and re-layouts  1.77 us (3%)
    all_to_all x2, blocking collectives, exchange(): return lax.all_to_all(value, axis, split_axis=0, concat_axis=0, tiled=True)  51.5 us
    pallas_call x1, Pallas kernels, time_section(): pl.pallas_call(time_kernel, out_shape=[pltpu.VMEM((2 * rows, width), bf16...  7.1 us
    ppermute x1, waiting for transfers between devices, on_device(): taken = lax.ppermute(given, 'segment', [(0, 1), (1, 0)])  2.26 us
    ppermute x1, starting transfers between devices, on_device(): w_in_first = lax.ppermute(w_in_sent, 'segment', [(0, 1)])  2.2 us
    unnamed x7, local copies, waits for them, and re-layouts  1.77 us
    ppermute x1, starting transfers between devices, on_device(): w_back_first = lax.ppermute(w_back_sent, 'segment', [(0, 1)])  1.44 us
  transfers between devices with their start and end apart: 3, of which 1 were waited for; matrix products, arithmetic and copies ran while one was open for 0% of the time, Pallas kernels for 0%

profile of v3, /device:TPU:8, one launch (start us, length us, event | category | flops | bytes accessed | tf_op | source)
XLA Modules:
  0.0 67.8 jit_solution(909226072200017433)
XLA Ops:
  0.0 1.3 %spread.1 = bf16[256,1536]{1,0:T(8,128)(2,1)S(1)} custom-call(s32[1]{0:T(128)} %bitcast.6.half, bf16[8,64,1536]{2,1,0:T(8,128)(2,1)} %bitcast.19), custom_call_target="tpu_custom_call" | custom-call | tf_op jit(solution)/shard_map/spread/pallas_call | solution.py:74
  1.3 2.2 %collective-permute-start = (bf16[1536,2304]{1,0:T(8,128)(2,1)}, bf16[1536,2304]{1,0:T(8,128)(2,1)S(1)}, u32[]{:S(2)}, u32[]{:S(2)}) collective-permute-start(bf16[1536,2304]{1,0:T(8,128)(2,1)} %bitcast.16), channel_id=1, source_target_pairs={{0,128},{1,129},{2,130},{3,131},{4,132},{5,133},{6,134},{7,135},{8... | collective-permute-start | bytes 21233672 | tf_op jit(solution)/shard_map/ppermute | solution.py:376
  3.5 1.4 %collective-permute-start.1 = (bf16[768,1536]{1,0:T(8,128)(2,1)}, bf16[768,1536]{1,0:T(8,128)(2,1)S(1)}, u32[]{:S(2)}, u32[]{:S(2)}) collective-permute-start(bf16[768,1536]{1,0:T(8,128)(2,1)} %bitcast.10.back_own), channel_id=1, source_target_pairs={{0,128},{1,129},{2,130},{3,131},{4,132},{5,133},{6,134},{7,135},{8... | collective-permute-start | bytes 7077896 | tf_op jit(solution)/shard_map/ppermute | solution.py:377
  5.0 18.7 %all_to_all.14 = bf16[16,16,1536]{2,1,0:T(8,128)(2,1)S(1)} all-to-all(bf16[16,16,1536]{2,1,0:T(8,128)(2,1)S(1)} %bitcast.15), channel_id=1, replica_groups=mesh['segment'=2,'z'=8,'plane'=16] {'plane'}, dimensions={0} | all-to-all | bytes 1572864 | tf_op jit(solution)/shard_map/all_to_all | solution.py:358
  23.7 0.0 collective-permute-done.1.back_sent
  23.7 0.0 copy-start
  23.7 0.0 collective-permute-done.sent_hbm
  23.7 7.1 %time_section.1 = (bf16[512,1536]{1,0:T(8,128)(2,1)S(1)}, bf16[16,32,768]{2,1,0:T(8,128)(2,1)}, bf16[16,16,1536]{2,1,0:T(8,128)(2,1)S(1)}) custom-call(s32[1]{0:T(128)} %bitcast.6.half, bf16[256,1536]{1,0:T(8,128)(2,1)S(1)} %bitcast.14, bf16[1536,2304]{1,0:T(8,128)(2,1)} %bitcast.17, bf16[1536,2304]{1,0:T(8,128)(2,1)S(1)} %collective-permute-done.sent_hbm, ...), custom_call_target="tpu_custom_call" | custom-call | tf_op jit(solution)/shard_map/time_section/pallas_call | solution.py:192
  30.8 0.0 copy-done
  30.8 0.1 collective-permute-start.2
  30.9 2.3 %collective-permute-done.2.part_ref = bf16[16,16,1536]{2,1,0:T(8,128)(2,1)S(1)} collective-permute-done((bf16[16,16,1536]{2,1,0:T(8,128)(2,1)S(1)}, bf16[16,16,1536]{2,1,0:T(8,128)(2,1)S(1)}, u32[]{:S(2)}, u32[]{:S(2)}) %collective-permute-start.2) | collective-permute-done | bytes 786464 | tf_op jit(solution)/shard_map/ppermute | solution.py:379
  33.2 0.0 copy-start.2
  33.2 0.0 copy-start.3
  33.2 0.1 join.1
  33.3 0.6 copy-done.2
  33.9 0.0 copy-done.3
  33.9 32.8 %conditional.1 = (bf16[1,1,1,512,1536]{4,3,2,1,0:T(8,128)(2,1)S(1)}) conditional(s32[]{:T(128)} %convert_element_type.3, (s32[]{:T(128)}, s32[1,8,4,2]{1,3,2,0:T(2,128)S(1)}, bf16[16,32,768]{2,1,0:T(8,128)(2,1)}, s32[1,1,512]{2,1,0:T(1,128)S(1)}, bf16[1,1,512,1536]{3,2,1,0:T(8,128)(2,1)}, /*index=5*/bf16[768,1536]{1,0:T(8,128)(2,1)}, ...), branch_computations={%region_0.1_spmd, %region_1.2_spmd} | conditional | flops 3 | bytes 8651498 | solution.py:389
  33.9 32.8 %all_to_all.13 = bf16[8,64,1536]{2,1,0:T(8,128)(2,1)S(1)} all-to-all(bf16[8,64,1536]{2,1,0:T(8,128)(2,1)S(1)} %bitcast.12), channel_id=1, replica_groups=mesh['segment'=2,'z'=8,'plane'=16] {'z'}, dimensions={0} | all-to-all | bytes 3145728 | tf_op jit(solution)/shard_map/cond/branch_1_fun/all_to_all | solution.py:358
  66.6 1.1 %copy.19 = bf16[1,1,1,512,1536]{4,3,2,1,0:T(8,128)(2,1)} copy(bf16[1,1,1,512,1536]{4,3,2,1,0:T(8,128)(2,1)S(1)} %get-tuple-element.62) | data formatting | bytes 3145728
Async XLA Ops:
  1.3 22.4 %collective-permute-start = (bf16[1536,2304]{1,0:T(8,128)(2,1)}, bf16[1536,2304]{1,0:T(8,128)(2,1)S(1)}, u32[]{:S(2)}, u32[]{:S(2)}) collective-permute-start(bf16[1536,2304]{1,0:T(8,128)(2,1)} %bitcast.16), channel_id=1, source_target_pairs={{0,128},{1,129},{2,130},{3,131},{4,132},{5,133},{6,134},{7,135},{8... | collective-permute-start | bytes 21233672 | tf_op jit(solution)/shard_map/ppermute | solution.py:376
  3.5 20.2 %collective-permute-start.1 = (bf16[768,1536]{1,0:T(8,128)(2,1)}, bf16[768,1536]{1,0:T(8,128)(2,1)S(1)}, u32[]{:S(2)}, u32[]{:S(2)}) collective-permute-start(bf16[768,1536]{1,0:T(8,128)(2,1)} %bitcast.10.back_own), channel_id=1, source_target_pairs={{0,128},{1,129},{2,130},{3,131},{4,132},{5,133},{6,134},{7,135},{8... | collective-permute-start | bytes 7077896 | tf_op jit(solution)/shard_map/ppermute | solution.py:377
  23.7 7.1 %copy-start = (bf16[768,1536]{1,0:T(8,128)(2,1)}, bf16[768,1536]{1,0:T(8,128)(2,1)S(1)}, u32[]{:S(2)}) copy-start(bf16[768,1536]{1,0:T(8,128)(2,1)S(1)} %collective-permute-done.1.back_sent) | copy-start | bytes 7077892
  30.8 2.4 %collective-permute-start.2 = (bf16[16,16,1536]{2,1,0:T(8,128)(2,1)S(1)}, bf16[16,16,1536]{2,1,0:T(8,128)(2,1)S(1)}, u32[]{:S(2)}, u32[]{:S(2)}) collective-permute-start(bf16[16,16,1536]{2,1,0:T(8,128)(2,1)S(1)} %get-tuple-element.57), channel_id=1, source_target_pairs={{0,128},{128,0},{1,129},{129,1},{2,130},{130,2},{3,131},{131,3},{4... | collective-permute-start | bytes 2359304 | tf_op jit(solution)/shard_map/ppermute | solution.py:379
  33.2 0.7 %copy-start.2 = (s32[1,8,4,2]{1,3,2,0:T(2,128)S(1)}, s32[1,8,4,2]{1,3,2,0:T(2,128)}, u32[]{:S(2)}) copy-start(s32[1,8,4,2]{1,3,2,0:T(2,128)} %param.11) | copy-start | bytes 772
  33.2 0.7 %copy-start.3 = (s32[1,1,512]{2,1,0:T(1,128)S(1)}, s32[1,1,512]{2,1,0:T(1,128)}, u32[]{:S(2)}) copy-start(s32[1,1,512]{2,1,0:T(1,128)} %param.10) | copy-start | bytes 6148

commit v4 on v3

--- a/solution.py
+++ b/solution.py
@@ -138,9 +138,11 @@
     get_w = qkv_copies(own_hbm, w, sem_w)
     for pair in range(PAIRS):
         parts = []
-        for get in get_w[pair * 3 : pair * 3 + 3]:
+        for get in get_w[pair * 3 : pair * 3 + 3] if pair else ():
             get.wait()
         for part in range(3):
+            if pair == 0:
+                get_w[part].wait()
             at = part * INNER + pair * PAIR
             y = jnp.dot(x, w[:, at : at + PAIR], preferred_element_type=f32) * factor
             parts.append(y.reshape(FRAMES, tracks, PAIR))
@@ -256,7 +258,7 @@
 
 def track_kernel(
     planes, lists, m_ref, seen_ref, x_hbm, w0_hbm, wq_hbm, w1_hbm, o_ref,
-    x_buf, w0, wq, w1, mixed0, first, qkv_0, qkv_1, qkv_2, mixed1, sem_more,
+    x_buf, w0, wq, w1, mixed0, first, qkv_0, qkv_1, qkv_2, mixed1, bias, sem_more,
 ):
     rows = x_buf.shape[0]
     blocks = rows // BLOCK
@@ -275,53 +277,42 @@
     itself = lax.broadcasted_iota(jnp.int32, (BLOCK, BLOCK), 0) == lax.broadcasted_iota(
         jnp.int32, (BLOCK, BLOCK), 1
     )
+    for block in range(blocks):
+        for other in range(blocks):
+            seen = seen_ref[other : other + 1, :] == 1
+            if other == block:
+                penalty = jnp.where(seen | itself, 0.0, LOW)
+            else:
+                listed = (lists[block * 2] == other) | (lists[block * 2 + 1] == other)
+                row = jnp.where(seen, jnp.where(listed, 0.0, LOW), LOW)
+                penalty = jnp.broadcast_to(row, (BLOCK, BLOCK))
+            at = (slice(block * BLOCK, (block + 1) * BLOCK), slice(other * BLOCK, (other + 1) * BLOCK))
+            bias[at] = penalty
     get_wq.wait()
     for pair, qkv in enumerate((qkv_0, qkv_1, qkv_2)):
         for part in range(3):
             at = part * INNER + pair * PAIR
             y = jnp.dot(first[...], wq[:, at : at + PAIR], preferred_element_type=f32) * factor
             qkv[:, part * PAIR : (part + 1) * PAIR] = y.astype(bf16)
-        for head in range(2):
-            at = head * HDIM
-            out_at = (pair * 2 + head) * HDIM
-            groups = []
-            for block in range(blocks):
-                others = [lists[block * 2], lists[block * 2 + 1]]
-                places = [pl.ds(block * BLOCK, BLOCK)] + [
-                    pl.ds(pl.multiple_of(o * BLOCK, BLOCK), BLOCK) for o in others
-                ]
-                allowed = [(seen_ref[block : block + 1, :] == 1) | itself] + [
-                    seen_ref[pl.ds(o, 1), :] == 1 for o in others
-                ]
-                q = qkv[pl.ds(block * BLOCK, BLOCK), at : at + HDIM]
-                groups.append((q, places, allowed))
-            scores = [
-                [
-                    jnp.where(allow, similar(q, qkv[place, PAIR + at : PAIR + at + HDIM]), LOW)
-                    for place, allow in zip(places, allowed)
-                ]
-                for q, places, allowed in groups
-            ]
-            tops = [
-                jnp.max(functools.reduce(jnp.maximum, ss), axis=-1, keepdims=True) for ss in scores
-            ]
-            es = [[jnp.exp2((s - top) * SCALE) for s in ss] for ss, top in zip(scores, tops)]
-            totals = [jnp.sum(sum(e[1:], e[0]), axis=-1, keepdims=True) for e in es]
-            sums = [
-                sum(
-                    jnp.dot(
-                        e.astype(bf16),
-                        qkv[place, 2 * PAIR + at : 2 * PAIR + at + HDIM],
-                        preferred_element_type=f32,
-                    )
-                    for e, place in zip(parts, places)
-                )
-                for parts, (q, places, allowed) in zip(es, groups)
-            ]
-            for block, (total, mixed) in enumerate(zip(totals, sums)):
-                mixed1[block * BLOCK : (block + 1) * BLOCK, out_at : out_at + HDIM] = (
-                    mixed * (1.0 / total)
-                ).astype(bf16)
+        ats = [head * HDIM for head in range(2)]
+        scores = [
+            similar(qkv[:, at : at + HDIM], qkv[:, PAIR + at : PAIR + at + HDIM]) + bias[...]
+            for at in ats
+        ]
+        tops = [jnp.max(s, axis=-1, keepdims=True) for s in scores]
+        es = [jnp.exp2((s - top) * SCALE) for s, top in zip(scores, tops)]
+        totals = [jnp.sum(e, axis=-1, keepdims=True) for e in es]
+        sums = [
+            jnp.dot(
+                e.astype(bf16),
+                qkv[:, 2 * PAIR + at : 2 * PAIR + at + HDIM],
+                preferred_element_type=f32,
+            )
+            for e, at in zip(es, ats)
+        ]
+        for at, total, summed in zip(ats, totals, sums):
+            out_at = pair * PAIR + at
+            mixed1[:, out_at : out_at + HDIM] = (summed * (1.0 / total)).astype(bf16)
     get_w1.wait()
     delta = jnp.dot(mixed1[...], w1[...], preferred_element_type=f32)
     o_ref[...] = (first[...].astype(f32) + delta).astype(bf16)
@@ -347,6 +338,7 @@
             pltpu.VMEM((rows, 3 * PAIR), bf16),
             pltpu.VMEM((rows, 3 * PAIR), bf16),
             pltpu.VMEM((rows, INNER), bf16),
+            pltpu.VMEM((rows, rows), f32),
             pltpu.SemaphoreType.DMA((4,)),
         ],
         compiler_params=pltpu.CompilerParams(vmem_limit_bytes=40 << 20),

time: 68.1 us -> 68 us (level)
  no operation moved by 1% of the time
where the time goes in v4:
time: 68 us; the launch traced here: 67.7 us
  blocking collectives  51.5 us (76%)
  Pallas kernels  8.37 us (12%)
  starting transfers between devices  3.73 us (5%)
  waiting for transfers between devices  2.27 us (3%)
  local copies, waits for them, and re-layouts  1.77 us (3%)
    all_to_all x2, blocking collectives, exchange(): return lax.all_to_all(value, axis, split_axis=0, concat_axis=0, tiled=True)  51.5 us
    pallas_call x1, Pallas kernels, time_section(): pl.pallas_call(time_kernel, out_shape=[pltpu.VMEM((2 * rows, width), bf16...  7 us
    ppermute x1, waiting for transfers between devices, on_device(): taken = lax.ppermute(given, 'segment', [(0, 1), (1, 0)])  2.26 us
    ppermute x1, starting transfers between devices, on_device(): w_in_first = lax.ppermute(w_in_sent, 'segment', [(0, 1)])  2.2 us
    unnamed x7, local copies, waits for them, and re-layouts  1.77 us
    ppermute x1, starting transfers between devices, on_device(): w_back_first = lax.ppermute(w_back_sent, 'segment', [(0, 1)])  1.44 us
  transfers between devices with their start and end apart: 3, of which 1 were waited for; matrix products, arithmetic and copies ran while one was open for 0% of the time, Pallas kernels for 0%

profile of v4, /device:TPU:8, one launch (start us, length us, event | category | flops | bytes accessed | tf_op | source)
XLA Modules:
  0.0 67.7 jit_solution(12444421404565653505)
XLA Ops:
  0.0 1.3 %spread.1 = bf16[256,1536]{1,0:T(8,128)(2,1)S(1)} custom-call(s32[1]{0:T(128)} %bitcast.6.half, bf16[8,64,1536]{2,1,0:T(8,128)(2,1)} %bitcast.19), custom_call_target="tpu_custom_call" | custom-call | tf_op jit(solution)/shard_map/spread/pallas_call | solution.py:74
  1.3 2.2 %collective-permute-start = (bf16[1536,2304]{1,0:T(8,128)(2,1)}, bf16[1536,2304]{1,0:T(8,128)(2,1)S(1)}, u32[]{:S(2)}, u32[]{:S(2)}) collective-permute-start(bf16[1536,2304]{1,0:T(8,128)(2,1)} %bitcast.16), channel_id=1, source_target_pairs={{0,128},{1,129},{2,130},{3,131},{4,132},{5,133},{6,134},{7,135},{8... | collective-permute-start | bytes 21233672 | tf_op jit(solution)/shard_map/ppermute | solution.py:368
  3.5 1.4 %collective-permute-start.1 = (bf16[768,1536]{1,0:T(8,128)(2,1)}, bf16[768,1536]{1,0:T(8,128)(2,1)S(1)}, u32[]{:S(2)}, u32[]{:S(2)}) collective-permute-start(bf16[768,1536]{1,0:T(8,128)(2,1)} %bitcast.10.back_own), channel_id=1, source_target_pairs={{0,128},{1,129},{2,130},{3,131},{4,132},{5,133},{6,134},{7,135},{8... | collective-permute-start | bytes 7077896 | tf_op jit(solution)/shard_map/ppermute | solution.py:369
  5.0 18.7 %all_to_all.14 = bf16[16,16,1536]{2,1,0:T(8,128)(2,1)S(1)} all-to-all(bf16[16,16,1536]{2,1,0:T(8,128)(2,1)S(1)} %bitcast.15), channel_id=1, replica_groups=mesh['segment'=2,'z'=8,'plane'=16] {'plane'}, dimensions={0} | all-to-all | bytes 1572864 | tf_op jit(solution)/shard_map/all_to_all | solution.py:350
  23.7 0.0 collective-permute-done.1.back_sent
  23.7 0.0 copy-start
  23.7 0.0 collective-permute-done.sent_hbm
  23.7 7.0 %time_section.1 = (bf16[512,1536]{1,0:T(8,128)(2,1)S(1)}, bf16[16,32,768]{2,1,0:T(8,128)(2,1)}, bf16[16,16,1536]{2,1,0:T(8,128)(2,1)S(1)}) custom-call(s32[1]{0:T(128)} %bitcast.6.half, bf16[256,1536]{1,0:T(8,128)(2,1)S(1)} %bitcast.14, bf16[1536,2304]{1,0:T(8,128)(2,1)} %bitcast.17, bf16[1536,2304]{1,0:T(8,128)(2,1)S(1)} %collective-permute-done.sent_hbm, ...), custom_call_target="tpu_custom_call" | custom-call | tf_op jit(solution)/shard_map/time_section/pallas_call | solution.py:194
  30.7 0.0 copy-done
  30.7 0.1 collective-permute-start.2
  30.8 2.3 %collective-permute-done.2.part_ref = bf16[16,16,1536]{2,1,0:T(8,128)(2,1)S(1)} collective-permute-done((bf16[16,16,1536]{2,1,0:T(8,128)(2,1)S(1)}, bf16[16,16,1536]{2,1,0:T(8,128)(2,1)S(1)}, u32[]{:S(2)}, u32[]{:S(2)}) %collective-permute-start.2) | collective-permute-done | bytes 786464 | tf_op jit(solution)/shard_map/ppermute | solution.py:371
  33.1 0.0 copy-start.2
  33.1 0.0 copy-start.3
  33.1 0.1 join.1
  33.2 0.6 copy-done.2
  33.8 0.0 copy-done.3
  33.8 32.8 %conditional.1 = (bf16[1,1,1,512,1536]{4,3,2,1,0:T(8,128)(2,1)S(1)}) conditional(s32[]{:T(128)} %convert_element_type.3, (s32[]{:T(128)}, s32[1,8,4,2]{1,3,2,0:T(2,128)S(1)}, bf16[16,32,768]{2,1,0:T(8,128)(2,1)}, s32[1,1,512]{2,1,0:T(1,128)S(1)}, bf16[1,1,512,1536]{3,2,1,0:T(8,128)(2,1)}, /*index=5*/bf16[768,1536]{1,0:T(8,128)(2,1)}, ...), branch_computations={%region_0.1_spmd, %region_1.2_spmd} | conditional | flops 3 | bytes 8651498 | solution.py:381
  33.8 32.8 %all_to_all.13 = bf16[8,64,1536]{2,1,0:T(8,128)(2,1)S(1)} all-to-all(bf16[8,64,1536]{2,1,0:T(8,128)(2,1)S(1)} %bitcast.12), channel_id=1, replica_groups=mesh['segment'=2,'z'=8,'plane'=16] {'z'}, dimensions={0} | all-to-all | bytes 3145728 | tf_op jit(solution)/shard_map/cond/branch_1_fun/all_to_all | solution.py:350
  66.6 1.1 %copy.19 = bf16[1,1,1,512,1536]{4,3,2,1,0:T(8,128)(2,1)} copy(bf16[1,1,1,512,1536]{4,3,2,1,0:T(8,128)(2,1)S(1)} %get-tuple-element.62) | data formatting | bytes 3145728
Async XLA Ops:
  1.3 22.4 %collective-permute-start = (bf16[1536,2304]{1,0:T(8,128)(2,1)}, bf16[1536,2304]{1,0:T(8,128)(2,1)S(1)}, u32[]{:S(2)}, u32[]{:S(2)}) collective-permute-start(bf16[1536,2304]{1,0:T(8,128)(2,1)} %bitcast.16), channel_id=1, source_target_pairs={{0,128},{1,129},{2,130},{3,131},{4,132},{5,133},{6,134},{7,135},{8... | collective-permute-start | bytes 21233672 | tf_op jit(solution)/shard_map/ppermute | solution.py:368
  3.5 20.2 %collective-permute-start.1 = (bf16[768,1536]{1,0:T(8,128)(2,1)}, bf16[768,1536]{1,0:T(8,128)(2,1)S(1)}, u32[]{:S(2)}, u32[]{:S(2)}) collective-permute-start(bf16[768,1536]{1,0:T(8,128)(2,1)} %bitcast.10.back_own), channel_id=1, source_target_pairs={{0,128},{1,129},{2,130},{3,131},{4,132},{5,133},{6,134},{7,135},{8... | collective-permute-start | bytes 7077896 | tf_op jit(solution)/shard_map/ppermute | solution.py:369
  23.7 7.0 %copy-start = (bf16[768,1536]{1,0:T(8,128)(2,1)}, bf16[768,1536]{1,0:T(8,128)(2,1)S(1)}, u32[]{:S(2)}) copy-start(bf16[768,1536]{1,0:T(8,128)(2,1)S(1)} %collective-permute-done.1.back_sent) | copy-start | bytes 7077892
  30.7 2.4 %collective-permute-start.2 = (bf16[16,16,1536]{2,1,0:T(8,128)(2,1)S(1)}, bf16[16,16,1536]{2,1,0:T(8,128)(2,1)S(1)}, u32[]{:S(2)}, u32[]{:S(2)}) collective-permute-start(bf16[16,16,1536]{2,1,0:T(8,128)(2,1)S(1)} %get-tuple-element.57), channel_id=1, source_target_pairs={{0,128},{128,0},{1,129},{129,1},{2,130},{130,2},{3,131},{131,3},{4... | collective-permute-start | bytes 2359304 | tf_op jit(solution)/shard_map/ppermute | solution.py:371
  33.1 0.7 %copy-start.2 = (s32[1,8,4,2]{1,3,2,0:T(2,128)S(1)}, s32[1,8,4,2]{1,3,2,0:T(2,128)}, u32[]{:S(2)}) copy-start(s32[1,8,4,2]{1,3,2,0:T(2,128)} %param.11) | copy-start | bytes 772
  33.1 0.7 %copy-start.3 = (s32[1,1,512]{2,1,0:T(1,128)S(1)}, s32[1,1,512]{2,1,0:T(1,128)}, u32[]{:S(2)}) copy-start(s32[1,1,512]{2,1,0:T(1,128)} %param.10) | copy-start | bytes 6148

commit v5 on v4

--- a/solution.py
+++ b/solution.py
@@ -68,7 +68,7 @@
         )
 
 
-def spread(x, half, planes, pieces=4):
+def spread(x, half, planes, pieces=2):
     rows, width = x.shape
     each = rows // planes
     return pl.pallas_call(

time: 68 us -> 67.9 us (level)
  no operation moved by 1% of the time
where the time goes in v5:
time: 67.9 us; the launch traced here: 67.6 us
  blocking collectives  51.5 us (76%)
  Pallas kernels  8.29 us (12%)
  starting transfers between devices  3.73 us (5%)
  waiting for transfers between devices  2.27 us (3%)
  local copies, waits for them, and re-layouts  1.77 us (3%)
    all_to_all x2, blocking collectives, exchange(): return lax.all_to_all(value, axis, split_axis=0, concat_axis=0, tiled=True)  51.5 us
    pallas_call x1, Pallas kernels, time_section(): pl.pallas_call(time_kernel, out_shape=[pltpu.VMEM((2 * rows, width), bf16...  7 us
    ppermute x1, waiting for transfers between devices, on_device(): taken = lax.ppermute(given, 'segment', [(0, 1), (1, 0)])  2.26 us
    ppermute x1, starting transfers between devices, on_device(): w_in_first = lax.ppermute(w_in_sent, 'segment', [(0, 1)])  2.2 us
    unnamed x7, local copies, waits for them, and re-layouts  1.77 us
    ppermute x1, starting transfers between devices, on_device(): w_back_first = lax.ppermute(w_back_sent, 'segment', [(0, 1)])  1.44 us
  transfers between devices with their start and end apart: 3, of which 1 were waited for; matrix products, arithmetic and copies ran while one was open for 0% of the time, Pallas kernels for 0%

profile of v5, /device:TPU:8, one launch (start us, length us, event | category | flops | bytes accessed | tf_op | source)
XLA Modules:
  0.0 67.6 jit_solution(13128387317908784128)
XLA Ops:
  0.0 1.2 %spread.1 = bf16[256,1536]{1,0:T(8,128)(2,1)S(1)} custom-call(s32[1]{0:T(128)} %bitcast.6.half, bf16[8,64,1536]{2,1,0:T(8,128)(2,1)} %bitcast.19), custom_call_target="tpu_custom_call" | custom-call | tf_op jit(solution)/shard_map/spread/pallas_call | solution.py:74
  1.2 2.2 %collective-permute-start = (bf16[1536,2304]{1,0:T(8,128)(2,1)}, bf16[1536,2304]{1,0:T(8,128)(2,1)S(1)}, u32[]{:S(2)}, u32[]{:S(2)}) collective-permute-start(bf16[1536,2304]{1,0:T(8,128)(2,1)} %bitcast.16), channel_id=1, source_target_pairs={{0,128},{1,129},{2,130},{3,131},{4,132},{5,133},{6,134},{7,135},{8... | collective-permute-start | bytes 21233672 | tf_op jit(solution)/shard_map/ppermute | solution.py:368
  3.4 1.4 %collective-permute-start.1 = (bf16[768,1536]{1,0:T(8,128)(2,1)}, bf16[768,1536]{1,0:T(8,128)(2,1)S(1)}, u32[]{:S(2)}, u32[]{:S(2)}) collective-permute-start(bf16[768,1536]{1,0:T(8,128)(2,1)} %bitcast.10.back_own), channel_id=1, source_target_pairs={{0,128},{1,129},{2,130},{3,131},{4,132},{5,133},{6,134},{7,135},{8... | collective-permute-start | bytes 7077896 | tf_op jit(solution)/shard_map/ppermute | solution.py:369
  4.9 18.7 %all_to_all.14 = bf16[16,16,1536]{2,1,0:T(8,128)(2,1)S(1)} all-to-all(bf16[16,16,1536]{2,1,0:T(8,128)(2,1)S(1)} %bitcast.15), channel_id=1, replica_groups=mesh['segment'=2,'z'=8,'plane'=16] {'plane'}, dimensions={0} | all-to-all | bytes 1572864 | tf_op jit(solution)/shard_map/all_to_all | solution.py:350
  23.6 0.0 collective-permute-done.1.back_sent
  23.6 0.0 copy-start
  23.6 0.0 collective-permute-done.sent_hbm
  23.6 7.0 %time_section.1 = (bf16[512,1536]{1,0:T(8,128)(2,1)S(1)}, bf16[16,32,768]{2,1,0:T(8,128)(2,1)}, bf16[16,16,1536]{2,1,0:T(8,128)(2,1)S(1)}) custom-call(s32[1]{0:T(128)} %bitcast.6.half, bf16[256,1536]{1,0:T(8,128)(2,1)S(1)} %bitcast.14, bf16[1536,2304]{1,0:T(8,128)(2,1)} %bitcast.17, bf16[1536,2304]{1,0:T(8,128)(2,1)S(1)} %collective-permute-done.sent_hbm, ...), custom_call_target="tpu_custom_call" | custom-call | tf_op jit(solution)/shard_map/time_section/pallas_call | solution.py:194
  30.6 0.0 copy-done
  30.6 0.1 collective-permute-start.2
  30.7 2.3 %collective-permute-done.2.part_ref = bf16[16,16,1536]{2,1,0:T(8,128)(2,1)S(1)} collective-permute-done((bf16[16,16,1536]{2,1,0:T(8,128)(2,1)S(1)}, bf16[16,16,1536]{2,1,0:T(8,128)(2,1)S(1)}, u32[]{:S(2)}, u32[]{:S(2)}) %collective-permute-start.2) | collective-permute-done | bytes 786464 | tf_op jit(solution)/shard_map/ppermute | solution.py:371
  33.0 0.0 copy-start.2
  33.0 0.0 copy-start.3
  33.0 0.1 join.1
  33.1 0.6 copy-done.2
  33.7 0.0 copy-done.3
  33.7 32.8 %conditional.1 = (bf16[1,1,1,512,1536]{4,3,2,1,0:T(8,128)(2,1)S(1)}) conditional(s32[]{:T(128)} %convert_element_type.3, (s32[]{:T(128)}, s32[1,8,4,2]{1,3,2,0:T(2,128)S(1)}, bf16[16,32,768]{2,1,0:T(8,128)(2,1)}, s32[1,1,512]{2,1,0:T(1,128)S(1)}, bf16[1,1,512,1536]{3,2,1,0:T(8,128)(2,1)}, /*index=5*/bf16[768,1536]{1,0:T(8,128)(2,1)}, ...), branch_computations={%region_0.1_spmd, %region_1.2_spmd} | conditional | flops 3 | bytes 8651498 | solution.py:381
  33.7 32.8 %all_to_all.13 = bf16[8,64,1536]{2,1,0:T(8,128)(2,1)S(1)} all-to-all(bf16[8,64,1536]{2,1,0:T(8,128)(2,1)S(1)} %bitcast.12), channel_id=1, replica_groups=mesh['segment'=2,'z'=8,'plane'=16] {'z'}, dimensions={0} | all-to-all | bytes 3145728 | tf_op jit(solution)/shard_map/cond/branch_1_fun/all_to_all | solution.py:350
  66.5 1.1 %copy.19 = bf16[1,1,1,512,1536]{4,3,2,1,0:T(8,128)(2,1)} copy(bf16[1,1,1,512,1536]{4,3,2,1,0:T(8,128)(2,1)S(1)} %get-tuple-element.62) | data formatting | bytes 3145728
Async XLA Ops:
  1.2 22.4 %collective-permute-start = (bf16[1536,2304]{1,0:T(8,128)(2,1)}, bf16[1536,2304]{1,0:T(8,128)(2,1)S(1)}, u32[]{:S(2)}, u32[]{:S(2)}) collective-permute-start(bf16[1536,2304]{1,0:T(8,128)(2,1)} %bitcast.16), channel_id=1, source_target_pairs={{0,128},{1,129},{2,130},{3,131},{4,132},{5,133},{6,134},{7,135},{8... | collective-permute-start | bytes 21233672 | tf_op jit(solution)/shard_map/ppermute | solution.py:368
  3.4 20.2 %collective-permute-start.1 = (bf16[768,1536]{1,0:T(8,128)(2,1)}, bf16[768,1536]{1,0:T(8,128)(2,1)S(1)}, u32[]{:S(2)}, u32[]{:S(2)}) collective-permute-start(bf16[768,1536]{1,0:T(8,128)(2,1)} %bitcast.10.back_own), channel_id=1, source_target_pairs={{0,128},{1,129},{2,130},{3,131},{4,132},{5,133},{6,134},{7,135},{8... | collective-permute-start | bytes 7077896 | tf_op jit(solution)/shard_map/ppermute | solution.py:369
  23.6 7.0 %copy-start = (bf16[768,1536]{1,0:T(8,128)(2,1)}, bf16[768,1536]{1,0:T(8,128)(2,1)S(1)}, u32[]{:S(2)}) copy-start(bf16[768,1536]{1,0:T(8,128)(2,1)S(1)} %collective-permute-done.1.back_sent) | copy-start | bytes 7077892
  30.6 2.4 %collective-permute-start.2 = (bf16[16,16,1536]{2,1,0:T(8,128)(2,1)S(1)}, bf16[16,16,1536]{2,1,0:T(8,128)(2,1)S(1)}, u32[]{:S(2)}, u32[]{:S(2)}) collective-permute-start(bf16[16,16,1536]{2,1,0:T(8,128)(2,1)S(1)} %get-tuple-element.57), channel_id=1, source_target_pairs={{0,128},{128,0},{1,129},{129,1},{2,130},{130,2},{3,131},{131,3},{4... | collective-permute-start | bytes 2359304 | tf_op jit(solution)/shard_map/ppermute | solution.py:371
  33.0 0.7 %copy-start.2 = (s32[1,8,4,2]{1,3,2,0:T(2,128)S(1)}, s32[1,8,4,2]{1,3,2,0:T(2,128)}, u32[]{:S(2)}) copy-start(s32[1,8,4,2]{1,3,2,0:T(2,128)} %param.11) | copy-start | bytes 772
  33.0 0.7 %copy-start.3 = (s32[1,1,512]{2,1,0:T(1,128)S(1)}, s32[1,1,512]{2,1,0:T(1,128)}, u32[]{:S(2)}) copy-start(s32[1,1,512]{2,1,0:T(1,128)} %param.10) | copy-start | bytes 6148
